TPU v7x, 256 devices: a whole 4x4x8 slice. The times are simulated.
256 devices in a mesh: grp: 32 (over x_lo, z, core), mem: 8 (over x_hi, y).
Axes of the slice: x: 4 (x_hi: 2, x_lo: 2; x = x_hi * 2 + x_lo), y: 4, z: 8, core: 2. Of those that a mesh axis runs over, the one named last changes fastest.
Arguments:
- queries: bfloat16 [16384, 32, 128], P('grp', 'mem'), may hold values from -16 to 16
- suffix_kv: bfloat16 [16384, 2, 4, 128], P('grp'), may hold values from -8 to 8
- prefix_kv: bfloat16 [256, 2, 128, 4, 128], P('grp'), may hold values from -8 to 8
- out_weight: bfloat16 [4096, 2048], P('mem'), may hold values from -0.09375 to 0.09375
- node_blocks: int32 [84], replicated, may hold values from 1 to 32, 256 in all
- root_of: int32 [16], replicated, may hold values from 0 to 3
- mid_of: int32 [64], replicated, may hold values from 0 to 15
Outputs:
- mixed: bfloat16 [16384, 2048], P(('grp', 'mem'))
Inputs may be any that keep to these rules, and one draw needn't show every extreme that they name: `node_blocks`: some node has exactly 32 blocks, and all together have 256.
All inputs are finite; a program needn't handle non-finite values.
Results may differ from a plain program's by a relative error of at most 0.025.
Values may be sent and summed in bfloat16 or wider, within the bound.
A program may use at most 128 MiB of HBM per device.

v0:
```python
import jax
import jax.numpy as jnp
from jax import lax
from jax.sharding import PartitionSpec as P

QH = 32
KVH = 4
SUFFIX = 256


NEG = -1e30


def absorb(running, grouped, key_rows, value_rows, allowed):
    highest, totals, summed = running
    score_scale = grouped.shape[-1] ** (-0.5)
    scores = (
        jnp.einsum("skph,tkh->kpst", grouped, key_rows, preferred_element_type=jnp.float32)
        * score_scale
    )
    scores = jnp.where(allowed, scores, NEG)
    raised = jnp.maximum(highest, jnp.max(scores, axis=-1))
    factor = jnp.exp(highest - raised)
    weights = jnp.exp(scores - raised[..., None])
    totals = totals * factor + jnp.sum(weights, axis=-1)
    summed = summed * factor[..., None] + jnp.einsum(
        "kpst,tkh->kpsh",
        weights.astype(jnp.bfloat16),
        value_rows,
        preferred_element_type=jnp.float32,
    )
    return (raised, totals, summed)


def path_ranges(request_ids, node_blocks, root_of, mid_of):
    nodes_all = node_blocks.shape[0]
    middles_all = root_of.shape[0]
    leaves = mid_of.shape[0]
    roots_all = nodes_all - middles_all - leaves
    firsts = jnp.cumsum(node_blocks) - node_blocks
    middles = jnp.sum(
        jnp.where(jnp.arange(leaves)[None, :] == request_ids[:, None], mid_of[None, :], 0), axis=1
    )
    root_ids = jnp.sum(
        jnp.where(jnp.arange(middles_all)[None, :] == middles[:, None], root_of[None, :], 0), axis=1
    )
    path_nodes = jnp.stack(
        [root_ids, roots_all + middles, roots_all + middles_all + request_ids], axis=1
    )
    picked = jnp.arange(nodes_all)[None, None, :] == path_nodes[:, :, None]
    lower_end = jnp.sum(jnp.where(picked, firsts[None, None, :], 0), axis=2)
    upper_end = lower_end + jnp.sum(jnp.where(picked, node_blocks[None, None, :], 0), axis=2)
    return (lower_end, upper_end)


def visible_blocks(block_ids, lower_end, upper_end):
    inside = (block_ids[:, None] >= lower_end[None, :]) & (block_ids[:, None] < upper_end[None, :])
    return jnp.any(inside, axis=1)


def on_device(queries, suffix_kv, prefix_kv, out_weight, node_blocks, root_of, mid_of):
    group_index = lax.axis_index("grp")
    head_index = lax.axis_index("mem")
    tokens_dev, heads_dev, head_dim = queries.shape
    req_local = tokens_dev // SUFFIX
    group_size = QH // KVH
    kv_dev = max(1, heads_dev // group_size)
    per_kv = heads_dev // kv_dev
    kv_start = head_index * heads_dev // group_size
    own_blocks = prefix_kv.shape[0]
    block_tokens = prefix_kv.shape[2]
    prefix_part = lax.dynamic_slice_in_dim(prefix_kv, kv_start, kv_dev, 3)
    suffix_part = lax.dynamic_slice_in_dim(suffix_kv, kv_start, kv_dev, 2)
    grouped = queries.reshape(req_local, SUFFIX, kv_dev, per_kv, head_dim)
    request_ids = group_index * req_local + jnp.arange(req_local)
    lower_end, upper_end = path_ranges(request_ids, node_blocks, root_of, mid_of)
    causal = jnp.arange(SUFFIX)[:, None] >= jnp.arange(SUFFIX)[None, :]
    empty = (
        jnp.full((kv_dev, per_kv, SUFFIX), NEG, jnp.float32),
        jnp.zeros((kv_dev, per_kv, SUFFIX), jnp.float32),
        jnp.zeros((kv_dev, per_kv, SUFFIX, head_dim), jnp.float32),
    )

    def suffix_status(j, running):
        rows = suffix_part[j * SUFFIX : (j + 1) * SUFFIX]
        return absorb(running, grouped[j], rows[:, 0], rows[:, 1], causal)

    def keys_path():
        start_status = tuple((empty for j in range(req_local)))
        piece = lax.all_gather(prefix_part, "grp", axis=0, tiled=True)
        count = piece.shape[0]

        def turn(i, running):
            block = lax.dynamic_slice_in_dim(piece, i * own_blocks, own_blocks, 0)
            key_rows = block[:, 0].reshape(own_blocks * block_tokens, kv_dev, head_dim)
            value_rows = block[:, 1].reshape(own_blocks * block_tokens, kv_dev, head_dim)
            block_ids = i * own_blocks + jnp.arange(own_blocks)
            updated = []
            for j in range(req_local):
                seen = visible_blocks(block_ids, lower_end[j], upper_end[j])
                allowed = jnp.repeat(seen, block_tokens)[None, :]
                updated.append(
                    lax.cond(
                        jnp.any(seen),
                        lambda s: absorb(s, grouped[j], key_rows, value_rows, allowed),
                        lambda s: s,
                        running[j],
                    )
                )
            return tuple(updated)

        folded = lax.fori_loop(0, count // own_blocks, turn, start_status)
        return tuple((suffix_status(j, folded[j]) for j in range(req_local)))

    finished = keys_path()
    pieces = []
    for j in range(req_local):
        totals = finished[j][1]
        summed = finished[j][2]
        attended = (summed / totals[..., None]).astype(jnp.bfloat16)
        pieces.append(jnp.transpose(attended, (2, 0, 1, 3)).reshape(SUFFIX, heads_dev * head_dim))
    attention = jnp.concatenate(pieces, axis=0)
    rows = attention
    return lax.psum_scatter(
        jnp.dot(rows, out_weight, preferred_element_type=jnp.float32).astype(jnp.bfloat16),
        "mem",
        scatter_dimension=0,
        tiled=True,
    )


def solution(mesh):
    return jax.shard_map(
        on_device,
        mesh=mesh,
        in_specs=(
            P("grp", "mem", None),
            P("grp", None, None, None),
            P("grp", None, None, None, None),
            P("mem", None),
            P(),
            P(),
            P(),
        ),
        out_specs=P(("grp", "mem"), None),
        check_vma=False,
    )
```

profile of v0, /device:TPU:124, one launch (start us, length us, event | category | flops | bytes accessed | tf_op | source)
XLA Modules:
  0.0 365.0 jit_solution(6380691217852413714)
XLA Ops:
  6.6 3.0 constant_dynamic-slice_fusion.5
  11.9 1.7 constant_dynamic-slice_fusion.6
  13.9 1.4 fusion.80
  15.2 1.3 fusion.79
  16.5 96.7 %all-gather.2.cloned.1.call-done = bf16[256,2,128,1,128]{4,2,0,3,1:T(8,128)(2,1)} async-done(((bf16[8,2,128,1,128]{4,2,0,3,1:T(8,128)(2,1)}), bf16[256,2,128,1,128]{4,2,0,3,1:T(8,128)(2,1)}) %all-gather.2.cloned.1.call-update) | async-done | bytes 16777232 | tf_op jit(solution)/shard_map/all_gather | solution.py:90
  114.9 122.8 %while.23 = (s32[]{:T(128)}, f32[1,4,256]{2,1,0:T(4,128)S(1)}, f32[1,4,256]{2,1,0:T(4,128)S(1)}, f32[1,4,256,128]{3,2,1,0:T(8,128)}, f32[1,4,256]{2,1,0:T(4,128)...) while((s32[]{:T(128)}, f32[1,4,256]{2,1,0:T(4,128)S(1)}, ...), condition=%wide.region_18.19_spmd, body=%wide.region_5.18_spmd.sunk | while | flops 1097341184 | bytes 38413188 | solution.py:112
  115.6 1.1 constant_dynamic-slice_fusion.8
  117.3 4.1 %conditional.5 = ((f32[1,4,256]{2,1,0:T(4,128)S(1)}, f32[1,4,256]{2,1,0:T(4,128)S(1)}, f32[1,4,256,128]{3,2,1,0:T(8,128)})) conditional(s32[]{:T(128)} %convert_element_type.70, (f32[1,4,256]{2,1,0:T(4,128)S(1)}, f32[1,4,256]{2,1,0:T(4,128)S(1)}, f32[1,4,256,128]{3,2,1,0:T(8,128)}) %tuple.79, (pred[8,3]{0,1:T(4,128)(4,1)S(1)}, ...), branch_computations={%region_13.13_spmd, %region_14.17_spmd} | conditional | flops 548670464 | bytes 18681984 | solution.py:103
  119.1 1.5 fusion.31
  122.0 4.1 %conditional.4 = ((f32[1,4,256]{2,1,0:T(4,128)S(1)}, f32[1,4,256]{2,1,0:T(4,128)S(1)}, f32[1,4,256,128]{3,2,1,0:T(8,128)})) conditional(s32[]{:T(128)} %convert_element_type.69, (f32[1,4,256]{2,1,0:T(4,128)S(1)}, f32[1,4,256]{2,1,0:T(4,128)S(1)}, f32[1,4,256,128]{3,2,1,0:T(8,128)}) %tuple.77, (pred[8,3]{0,1:T(4,128)(4,1)S(1)}, ...), branch_computations={%region_7.7_spmd, %region_8.11_spmd} | conditional | flops 548670464 | bytes 18681984 | solution.py:103
  123.9 1.5 fusion.10
  126.9 1.1 constant_dynamic-slice_fusion.8
  129.9 1.1 constant_dynamic-slice_fusion.8
  133.0 1.1 constant_dynamic-slice_fusion.8
  136.1 1.1 constant_dynamic-slice_fusion.8
  139.1 1.1 constant_dynamic-slice_fusion.8
  142.2 1.1 constant_dynamic-slice_fusion.8
  145.3 1.1 constant_dynamic-slice_fusion.8
  147.6 4.1 %conditional.4 = ((f32[1,4,256]{2,1,0:T(4,128)S(1)}, f32[1,4,256]{2,1,0:T(4,128)S(1)}, f32[1,4,256,128]{3,2,1,0:T(8,128)})) conditional(s32[]{:T(128)} %convert_element_type.69, (f32[1,4,256]{2,1,0:T(4,128)S(1)}, f32[1,4,256]{2,1,0:T(4,128)S(1)}, f32[1,4,256,128]{3,2,1,0:T(8,128)}) %tuple.77, (pred[8,3]{0,1:T(4,128)(4,1)S(1)}, ...), branch_computations={%region_7.7_spmd, %region_8.11_spmd} | conditional | flops 548670464 | bytes 18681984 | solution.py:103
  149.4 1.5 fusion.10
  152.4 1.1 constant_dynamic-slice_fusion.8
  154.1 4.1 %conditional.5 = ((f32[1,4,256]{2,1,0:T(4,128)S(1)}, f32[1,4,256]{2,1,0:T(4,128)S(1)}, f32[1,4,256,128]{3,2,1,0:T(8,128)})) conditional(s32[]{:T(128)} %convert_element_type.70, (f32[1,4,256]{2,1,0:T(4,128)S(1)}, f32[1,4,256]{2,1,0:T(4,128)S(1)}, f32[1,4,256,128]{3,2,1,0:T(8,128)}) %tuple.79, (pred[8,3]{0,1:T(4,128)(4,1)S(1)}, ...), branch_computations={%region_13.13_spmd, %region_14.17_spmd} | conditional | flops 548670464 | bytes 18681984 | solution.py:103
  155.9 1.5 fusion.31
  159.6 1.1 constant_dynamic-slice_fusion.8
  162.7 1.1 constant_dynamic-slice_fusion.8
  165.7 1.1 constant_dynamic-slice_fusion.8
  168.8 1.1 constant_dynamic-slice_fusion.8
  171.9 1.1 constant_dynamic-slice_fusion.8
  174.2 4.1 %conditional.4 = ((f32[1,4,256]{2,1,0:T(4,128)S(1)}, f32[1,4,256]{2,1,0:T(4,128)S(1)}, f32[1,4,256,128]{3,2,1,0:T(8,128)})) conditional(s32[]{:T(128)} %convert_element_type.69, (f32[1,4,256]{2,1,0:T(4,128)S(1)}, f32[1,4,256]{2,1,0:T(4,128)S(1)}, f32[1,4,256,128]{3,2,1,0:T(8,128)}) %tuple.77, (pred[8,3]{0,1:T(4,128)(4,1)S(1)}, ...), branch_computations={%region_7.7_spmd, %region_8.11_spmd} | conditional | flops 548670464 | bytes 18681984 | solution.py:103
  176.0 1.5 fusion.10
  179.0 1.1 constant_dynamic-slice_fusion.8
  180.6 4.1 %conditional.5 = ((f32[1,4,256]{2,1,0:T(4,128)S(1)}, f32[1,4,256]{2,1,0:T(4,128)S(1)}, f32[1,4,256,128]{3,2,1,0:T(8,128)})) conditional(s32[]{:T(128)} %convert_element_type.70, (f32[1,4,256]{2,1,0:T(4,128)S(1)}, f32[1,4,256]{2,1,0:T(4,128)S(1)}, f32[1,4,256,128]{3,2,1,0:T(8,128)}) %tuple.79, (pred[8,3]{0,1:T(4,128)(4,1)S(1)}, ...), branch_computations={%region_13.13_spmd, %region_14.17_spmd} | conditional | flops 548670464 | bytes 18681984 | solution.py:103
  182.5 1.5 fusion.31
  186.2 1.1 constant_dynamic-slice_fusion.8
  189.2 1.1 constant_dynamic-slice_fusion.8
  192.3 1.1 constant_dynamic-slice_fusion.8
  195.4 1.1 constant_dynamic-slice_fusion.8
  198.5 1.1 constant_dynamic-slice_fusion.8
  201.5 1.1 constant_dynamic-slice_fusion.8
  207.7 1.1 constant_dynamic-slice_fusion.8
  210.8 1.1 constant_dynamic-slice_fusion.8
  237.7 2.1 copy.48
  239.8 2.0 copy.52
  241.8 1.4 fusion.52
  243.3 1.4 fusion.54
  244.7 1.7 fusion.51
  246.8 2.6 convolution_convert_fusion
  249.4 108.7 %reduce-scatter.2.cloned.1.call-done = bf16[64,2048]{1,0:T(8,128)(2,1)} async-done(((bf16[512,2048]{1,0:T(8,128)(2,1)}), bf16[64,2048]{1,0:T(8,128)(2,1)}) %reduce-scatter.2.cloned.1.call-update) | async-done | bytes 262160 | tf_op jit(solution)/shard_map/reduce_scatter | solution.py:124
  (275 shorter events, 53.9 us)
Async XLA Ops:
  6.5 240.2 %copy-start = (bf16[512,2048]{1,0:T(8,128)(2,1)S(1)}, bf16[512,2048]{1,0:T(8,128)(2,1)}, u32[]{:S(2)}) copy-start(bf16[512,2048]{1,0:T(8,128)(2,1)} %param.16) | copy-start | bytes 6291460
  6.5 4.0 %copy-start.8 = (s32[84]{0:T(128)S(1)}, s32[84]{0:T(128)}, u32[]{:S(2)}) copy-start(s32[84]{0:T(128)} %param.17) | copy-start | bytes 1012
  6.5 4.4 %copy-start.9 = (s32[64]{0:T(128)S(1)}, s32[64]{0:T(128)}, u32[]{:S(2)}) copy-start(s32[64]{0:T(128)} %param.19) | copy-start | bytes 772
  6.5 4.6 %copy-start.10 = (s32[16]{0:T(128)S(1)}, s32[16]{0:T(128)}, u32[]{:S(2)}) copy-start(s32[16]{0:T(128)} %param.18) | copy-start | bytes 196
  6.5 5.3 %copy-start.2 = (bf16[512,4,128]{2,1,0:T(4,128)(2,1)S(1)}, bf16[512,4,128]{2,1,0:T(4,128)(2,1)}, u32[]{:S(2)}) copy-start(bf16[512,4,128]{2,1,0:T(4,128)(2,1)} %param.13) | copy-start | bytes 1572868
  6.5 106.6 %all-gather.2.cloned.1.call-start = ((), (), s32[]{:S(2)}) async-start(), calls=%async_computation.1 | async-start | bytes 17301504 | tf_op jit(solution)/shard_map/all_gather | solution.py:90
  10.5 347.6 %reduce-scatter.2.cloned.1.call-start = ((), (), s32[]{:S(2)}) async-start(), calls=%async_computation.2 | async-start | bytes 2359296 | tf_op jit(solution)/shard_map/reduce_scatter | solution.py:124
  117.4 1.7 copy-start.5
  120.6 0.8 copy-start.6
  122.1 1.7 copy-start.3
  125.3 0.8 copy-start.4
  147.7 1.7 copy-start.3
  150.9 0.8 copy-start.4
  154.2 1.7 copy-start.5
  157.4 0.8 copy-start.6
  174.3 1.7 copy-start.3
  177.5 0.8 copy-start.4
  180.7 1.7 copy-start.5
  183.9 0.8 copy-start.6
  237.7 8.7 %copy-start.1 = (f32[1,4,256,256]{2,3,1,0:T(8,128)S(1)}, f32[1,4,256,256]{2,3,1,0:T(8,128)}, u32[]{:S(2)}) copy-start(f32[1,4,256,256]{2,3,1,0:T(8,128)} %get-tuple-element.359) | copy-start | bytes 3145732
  241.8 4.6 %copy-start.7 = (f32[1,4,256,128]{2,3,1,0:T(8,128)S(1)}, f32[1,4,256,128]{2,3,1,0:T(8,128)}, u32[]{:S(2)}) copy-start(f32[1,4,256,128]{2,3,1,0:T(8,128)} %copy.52) | copy-start | bytes 1572868
Sparse Core Ops, SparseCore 0:
  10.6 102.5 all-gather.1
  249.5 108.5 reduce-scatter.1
where the time goes:
time: 370 us; the launch traced here: 365 us
  waiting for transfers between devices  205 us (55%)
  local copies, waits for them, and re-layouts  51.5 us (14%)
  loops' own time  41.1 us (11%)
  other arithmetic  32.7 us (9%)
  matrix products  20.5 us (6%)
  between operations  13.6 us (4%)
    reduce_scatter x1, waiting for transfers between devices, on_device(): lax.psum_scatter(jnp.dot(rows, out_weight, preferred_element_type=jnp.flo...  109 us
    all_gather x1, waiting for transfers between devices, keys_path(): piece = lax.all_gather(prefix_part, 'grp', axis=0, tiled=True)  96.7 us
    another operation x1, loops' own time, keys_path(): folded = lax.fori_loop(0, count // own_blocks, turn, start_status)  39.9 us
    slice x32, local copies, waits for them, and re-layouts, turn(): block[:, 1].reshape(own_blocks * block_tokens, kv_dev, head_dim)  34 us
    reduce_or x32, other arithmetic, turn(): jnp.any(seen)  23 us
    dot_general x8, matrix products, absorb(): jnp.einsum('kpst,tkh->kpsh', weights.astype(jnp.bfloat16), value_rows, pr...  10.8 us
    reduce_sum x8, other arithmetic, absorb(): totals = totals * factor + jnp.sum(weights, axis=-1)  8.39 us
  transfers between devices with their start and end apart: 2, of which 2 were waited for; matrix products, arithmetic and copies ran while one was open for 2% of the time, Pallas kernels for 0%

commit v1 on v0

v1 whole, which is shorter than its diff:
```python
import functools

import jax
import jax.numpy as jnp
from jax import lax
from jax.experimental import pallas as pl
from jax.experimental.pallas import tpu as pltpu
from jax.sharding import PartitionSpec as P

QH = 32
KVH = 4
SUFFIX = 256
MOST_BLK = 32
NEG = -1e30
MESH = pl.DeviceIdType.MESH


def path_table(request_ids, node_blocks, root_of, mid_of):
    nodes_all = node_blocks.shape[0]
    middles_all = root_of.shape[0]
    leaves = mid_of.shape[0]
    roots_all = nodes_all - middles_all - leaves
    firsts = jnp.cumsum(node_blocks) - node_blocks
    middles = jnp.sum(
        jnp.where(jnp.arange(leaves)[None, :] == request_ids[:, None], mid_of[None, :], 0), axis=1
    )
    root_ids = jnp.sum(
        jnp.where(jnp.arange(middles_all)[None, :] == middles[:, None], root_of[None, :], 0), axis=1
    )
    path_nodes = jnp.stack(
        [root_ids, roots_all + middles, roots_all + middles_all + request_ids], axis=1
    )
    picked = jnp.arange(nodes_all)[None, None, :] == path_nodes[:, :, None]
    starts = jnp.sum(jnp.where(picked, firsts[None, None, :], 0), axis=2)
    counts = jnp.sum(jnp.where(picked, node_blocks[None, None, :], 0), axis=2)
    ends = jnp.cumsum(counts, axis=1)
    begins = ends - counts
    slots = jnp.arange(3 * MOST_BLK)[None, :]
    which = (slots >= ends[:, 0:1]).astype(jnp.int32) + (slots >= ends[:, 1:2]).astype(jnp.int32)
    which = jnp.minimum(which, 2)
    pick = jnp.arange(3)[None, None, :] == which[:, :, None]
    start_of = jnp.sum(jnp.where(pick, starts[:, None, :], 0), axis=2)
    begin_of = jnp.sum(jnp.where(pick, begins[:, None, :], 0), axis=2)
    ids = start_of + slots - begin_of
    total = ends[:, 2]
    ids = jnp.where(slots < total[:, None], ids, 0)
    return ids.astype(jnp.int32), total.astype(jnp.int32)


def attend_kernel(slots, ids_ref, cnt_ref, q_ref, ks_ref, vs_ref, kv_hbm, o_ref, buf, sem, m_sc, l_sc, acc_sc):
    j = pl.program_id(0)
    n = cnt_ref[j]
    rows, hd = q_ref.shape
    scale = hd ** (-0.5)
    contract = (((1,), (1,)), ((), ()))
    q = q_ref[...]

    scores = lax.dot_general(q, ks_ref[...], contract, preferred_element_type=jnp.float32) * scale
    tok = lax.broadcasted_iota(jnp.int32, scores.shape, 0) % SUFFIX
    key = lax.broadcasted_iota(jnp.int32, scores.shape, 1)
    scores = jnp.where(key <= tok, scores, NEG)
    high = jnp.max(scores, axis=-1, keepdims=True)
    weights = jnp.exp(scores - high)
    m_sc[...] = high
    l_sc[...] = jnp.sum(weights, axis=-1, keepdims=True)
    acc_sc[...] = jnp.dot(weights.astype(jnp.bfloat16), vs_ref[...], preferred_element_type=jnp.float32)

    def fetch(i, slot):
        pltpu.make_async_copy(kv_hbm.at[ids_ref[j * slots + i]], buf.at[slot], sem.at[slot]).start()

    @pl.when(n > 0)
    def _():
        fetch(0, 0)

    def body(i, carry):
        slot = i % 2
        pltpu.make_async_copy(kv_hbm.at[0], buf.at[slot], sem.at[slot]).wait()

        @pl.when(i + 1 < n)
        def _():
            fetch(i + 1, 1 - slot)

        s = lax.dot_general(q, buf[slot, 0], contract, preferred_element_type=jnp.float32) * scale
        m_old = m_sc[...]
        m_new = jnp.maximum(m_old, jnp.max(s, axis=-1, keepdims=True))
        factor = jnp.exp(m_old - m_new)
        p = jnp.exp(s - m_new)
        l_sc[...] = l_sc[...] * factor + jnp.sum(p, axis=-1, keepdims=True)
        acc_sc[...] = acc_sc[...] * factor + jnp.dot(
            p.astype(jnp.bfloat16), buf[slot, 1], preferred_element_type=jnp.float32
        )
        m_sc[...] = m_new
        return carry

    lax.fori_loop(0, n, body, 0)
    o_ref[...] = (acc_sc[...] / l_sc[...]).astype(o_ref.dtype)


def attend(ids, counts, q, ks, vs, kv_all):
    req, rows, hd = q.shape
    slots = ids.shape[1]
    block_shape = kv_all.shape[1:]
    return pl.pallas_call(
        functools.partial(attend_kernel, slots),
        out_shape=jax.ShapeDtypeStruct((req, rows, hd), jnp.bfloat16),
        grid_spec=pltpu.PrefetchScalarGridSpec(
            num_scalar_prefetch=2,
            grid=(req,),
            in_specs=[
                pl.BlockSpec((None, rows, hd), lambda j, ids, cnt: (j, 0, 0)),
                pl.BlockSpec((None, SUFFIX, hd), lambda j, ids, cnt: (j, 0, 0)),
                pl.BlockSpec((None, SUFFIX, hd), lambda j, ids, cnt: (j, 0, 0)),
                pl.BlockSpec(memory_space=pl.ANY),
            ],
            out_specs=pl.BlockSpec((None, rows, hd), lambda j, ids, cnt: (j, 0, 0)),
            scratch_shapes=[
                pltpu.VMEM((2,) + block_shape, kv_all.dtype),
                pltpu.SemaphoreType.DMA((2,)),
                pltpu.VMEM((rows, 1), jnp.float32),
                pltpu.VMEM((rows, 1), jnp.float32),
                pltpu.VMEM((rows, hd), jnp.float32),
            ],
        ),
        compiler_params=pltpu.CompilerParams(dimension_semantics=("arbitrary",)),
    )(ids.reshape(-1), counts, q, ks, vs, kv_all)


def exchange_kernel(n, x_ref, o_ref, recv, send_sem, recv_sem):
    me = lax.axis_index("mem")
    grp = lax.axis_index("grp")
    barrier = pltpu.get_barrier_semaphore()
    for k in range(1, n):
        pl.semaphore_signal(barrier, inc=1, device_id=(grp, lax.rem(me + k, n)), device_id_type=MESH)
    pl.semaphore_wait(barrier, n - 1)
    copies = []
    for k in range(1, n):
        peer = lax.rem(me + k, n)
        copy = pltpu.make_async_remote_copy(
            src_ref=x_ref.at[peer],
            dst_ref=recv.at[k],
            send_sem=send_sem.at[k],
            recv_sem=recv_sem.at[k],
            device_id=(grp, peer),
            device_id_type=MESH,
        )
        copy.start()
        copies.append(copy)
    total = x_ref[me].astype(jnp.float32)
    for k in range(1, n):
        copies[k - 1].wait()
        total = total + recv[k].astype(jnp.float32)
    o_ref[...] = total.astype(o_ref.dtype)


def exchange_sum(x):
    n, rows, cols = x.shape
    return pl.pallas_call(
        functools.partial(exchange_kernel, n),
        out_shape=jax.ShapeDtypeStruct((rows, cols), x.dtype),
        in_specs=[pl.BlockSpec(memory_space=pltpu.VMEM)],
        out_specs=pl.BlockSpec(memory_space=pltpu.VMEM),
        scratch_shapes=[
            pltpu.VMEM((n, rows, cols), x.dtype),
            pltpu.SemaphoreType.DMA((n,)),
            pltpu.SemaphoreType.DMA((n,)),
        ],
        compiler_params=pltpu.CompilerParams(collective_id=0, has_side_effects=True),
    )(x)


def on_device(n_mem, queries, suffix_kv, prefix_kv, out_weight, node_blocks, root_of, mid_of):
    group_index = lax.axis_index("grp")
    head_index = lax.axis_index("mem")
    tokens_dev, heads_dev, head_dim = queries.shape
    req_local = tokens_dev // SUFFIX
    group_size = QH // KVH
    kv_start = head_index * heads_dev // group_size
    prefix_part = lax.dynamic_index_in_dim(prefix_kv, kv_start, 3, keepdims=False)
    suffix_part = lax.dynamic_index_in_dim(suffix_kv, kv_start, 2, keepdims=False)
    kv_all = lax.all_gather(prefix_part, "grp", axis=0, tiled=True)

    request_ids = group_index * req_local + jnp.arange(req_local)
    ids, counts = path_table(request_ids, node_blocks, root_of, mid_of)

    q = queries.reshape(req_local, SUFFIX, heads_dev, head_dim).transpose(0, 2, 1, 3)
    q = q.reshape(req_local, heads_dev * SUFFIX, head_dim)
    ks = suffix_part[:, 0].reshape(req_local, SUFFIX, head_dim)
    vs = suffix_part[:, 1].reshape(req_local, SUFFIX, head_dim)
    attended = attend(ids, counts, q, ks, vs, kv_all)
    attended = attended.reshape(req_local, heads_dev, SUFFIX, head_dim)
    w = out_weight.reshape(heads_dev, head_dim, out_weight.shape[1])
    partial = lax.dot_general(
        attended, w, (((1, 3), (0, 1)), ((), ())), preferred_element_type=jnp.float32
    ).astype(jnp.bfloat16)
    partial = partial.reshape(tokens_dev, out_weight.shape[1])
    partial = partial.reshape(n_mem, tokens_dev // n_mem, out_weight.shape[1])
    return exchange_sum(partial)


def solution(mesh):
    return jax.shard_map(
        functools.partial(on_device, mesh.shape["mem"]),
        mesh=mesh,
        in_specs=(
            P("grp", "mem", None),
            P("grp", None, None, None),
            P("grp", None, None, None, None),
            P("mem", None),
            P(),
            P(),
            P(),
        ),
        out_specs=P(("grp", "mem"), None),
        check_vma=False,
    )
```

time: 370 us -> 232 us (0.63)
  the two profiles are of different devices: /device:TPU:124 before, /device:TPU:156 now
where the time goes in v1:
time: 232 us
  Pallas kernels  109 us (47%)
  waiting for transfers between devices  94.8 us (41%)
  between operations  13.5 us (6%)
  local copies, waits for them, and re-layouts  9.74 us (4%)
  matrix products  3.65 us (2%)
    all_gather x1, waiting for transfers between devices, on_device(): kv_all = lax.all_gather(prefix_part, 'grp', axis=0, tiled=True)  94.8 us
    pallas_call x1, Pallas kernels, attend(): pl.pallas_call(functools.partial(attend_kernel, slots), out_shape=jax.Sha...  83.8 us
    pallas_call x1, Pallas kernels, exchange_sum(): pl.pallas_call(functools.partial(exchange_kernel, n), out_shape=jax.Shape...  24.9 us
  transfers between devices with their start and end apart: 1, of which 1 were waited for; matrix products, arithmetic and copies ran while one was open for 2% of the time, Pallas kernels for 0%

profile of v1, /device:TPU:156, one launch (start us, length us, event | category | flops | bytes accessed | tf_op | source)
XLA Modules:
  0.0 231.6 jit_solution(17729731113331223529)
XLA Ops:
  6.5 0.0 copy-start
  6.5 0.0 all-gather.3.cloned.1.call-start
  6.5 3.0 %constant_dynamic-slice_fusion = bf16[8,2,128,1,128]{4,3,2,1,0:T(2,128)(2,1)S(1)} fusion(bf16[8,2,128,4,128]{4,3,2,1,0:T(4,128)(2,1)} %param.9, s32[]{:T(128)S(6)} %select_n.50), kind=kLoop, calls=%fused_computation.23 | loop fusion | bytes 1048580 | tf_op jit(solution)/shard_map/jit(dynamic_index_in_dim)/dynamic_slice | solution.py:178
  9.5 0.0 copy-start.3
  9.5 0.0 copy-start.4
  9.5 0.0 copy-start.5
  9.5 0.0 copy-start.1
  9.6 0.9 copy.31
  10.5 0.0 all-gather.3.cloned.1.call-update
  10.5 1.8 constant_dynamic-slice_fusion.1
  12.3 0.0 copy-done.3
  12.3 0.1 copy.25
  12.4 0.1 reduce-window.9
  12.6 0.1 reduce
  12.7 0.0 copy-done.4
  12.7 0.2 fusion
  12.9 0.0 copy-done.5
  12.9 0.2 fusion.1
  13.1 0.3 select_reduce_fusion.2
  13.4 0.0 copy-start.2
  13.4 0.1 fusion.3
  13.5 0.1 select_reduce_fusion.1
  13.6 0.1 compare_select_fusion
  13.7 0.7 select_n.48.ids_ref
  14.3 0.0 copy-done.1
  14.3 0.9 copy.26
  15.2 0.7 fusion.4
  15.9 94.8 %all-gather.3.cloned.1.call-done = bf16[256,2,128,1,128]{4,2,3,1,0:T(8,128)(2,1)} async-done(((bf16[8,2,128,1,128]{4,2,3,1,0:T(8,128)(2,1)}), bf16[256,2,128,1,128]{4,2,3,1,0:T(8,128)(2,1)}) %all-gather.3.cloned.1.call-update) | async-done | bytes 16777232 | tf_op jit(solution)/shard_map/all_gather | solution.py:180
  110.7 0.0 copy-done.2
  110.7 83.8 %shard_map.73 = bf16[2,1024,128]{2,1,0:T(8,128)(2,1)} custom-call(s32[192]{0:T(256)} %select_n.48.ids_ref, s32[2]{0:T(128)} %copy-done.2, bf16[2,1024,128]{2,1,0:T(8,128)(2,1)} %bitcast.32, bf16[2,256,128]{2,1,0:T(8,128)(2,1)} %bitcast.36, bf16[2,256,128]{2,1,0:T(8,128)(2,1)} %bitcast.35, bf16[256,2,128,128]{3,2,1,0:T(8,128)(2,1)} %bitcast.31), custom_call_target="tpu_custom_call" | custom-call | tf_op jit(solution)/shard_map/pallas_call | solution.py:103
  194.5 0.0 copy-done
  194.5 3.7 %bitcast_convert_fusion = bf16[2,256,2048]{2,1,0:T(8,128)(2,1)} fusion(bf16[2,4,256,128]{3,2,1,0:T(8,128)(2,1)} %bitcast.37, bf16[4,128,2048,1]{2,1,0,3:T(8,128)(2,1)S(1)} %bitcast.30), kind=kOutput, calls=%fused_computation | convolution fusion | flops 1074790400 | bytes 4718592 | tf_op jit(solution)/shard_map/dot_general | solution.py:192
  198.2 24.9 %shard_map.74 = bf16[64,2048]{1,0:T(8,128)(2,1)} custom-call(bf16[8,64,2048]{2,1,0:T(8,128)(2,1)} %bitcast.33), custom_call_target="tpu_custom_call" | custom-call | tf_op jit(solution)/shard_map/pallas_call | solution.py:157
  223.1 1.7 copy.35
  (9 shorter events, 0.1 us)
Async XLA Ops:
  6.5 188.0 %copy-start = (bf16[512,2048]{1,0:T(8,128)(2,1)S(1)}, bf16[512,2048]{1,0:T(8,128)(2,1)}, u32[]{:S(2)}) copy-start(bf16[512,2048]{1,0:T(8,128)(2,1)} %param.10) | copy-start | bytes 6291460
  6.5 104.2 %all-gather.3.cloned.1.call-start = ((), (), s32[]{:S(2)}) async-start(), calls=%async_computation | async-start | bytes 17301504 | tf_op jit(solution)/shard_map/all_gather | solution.py:180
  9.5 2.8 %copy-start.3 = (s32[84]{0:T(128)S(1)}, s32[84]{0:T(128)}, u32[]{:S(2)}) copy-start(s32[84]{0:T(128)} %param.11) | copy-start | bytes 1012
  9.5 3.2 %copy-start.4 = (s32[64]{0:T(128)S(1)}, s32[64]{0:T(128)}, u32[]{:S(2)}) copy-start(s32[64]{0:T(128)} %param.13) | copy-start | bytes 772
  9.5 3.4 %copy-start.5 = (s32[16]{0:T(128)S(1)}, s32[16]{0:T(128)}, u32[]{:S(2)}) copy-start(s32[16]{0:T(128)} %param.12) | copy-start | bytes 196
  9.5 4.8 %copy-start.1 = (bf16[512,4,128]{2,1,0:T(4,128)(2,1)S(1)}, bf16[512,4,128]{2,1,0:T(4,128)(2,1)}, u32[]{:S(2)}) copy-start(bf16[512,4,128]{2,1,0:T(4,128)(2,1)} %param.7) | copy-start | bytes 1572868
  13.4 97.3 %copy-start.2 = (s32[2]{0:T(128)}, s32[2]{0:T(128)S(1)}, u32[]{:S(2)}) copy-start(s32[2]{0:T(128)S(1)} %get-tuple-element.11.cnt_ref) | copy-start | bytes 28
Sparse Core Ops, SparseCore 0:
  10.6 100.0 all-gather.2

commit v2 on v1

--- a/solution.py
+++ b/solution.py
@@ -5,7 +5,7 @@
 from jax import lax
 from jax.experimental import pallas as pl
 from jax.experimental.pallas import tpu as pltpu
-from jax.sharding import PartitionSpec as P
+from jax.sharding import Mesh, PartitionSpec as P
 
 QH = 32
 KVH = 4
@@ -127,10 +127,10 @@
 
 def exchange_kernel(n, x_ref, o_ref, recv, send_sem, recv_sem):
     me = lax.axis_index("mem")
-    grp = lax.axis_index("grp")
+    grp = (lax.axis_index("chip"), lax.axis_index("core"))
     barrier = pltpu.get_barrier_semaphore()
     for k in range(1, n):
-        pl.semaphore_signal(barrier, inc=1, device_id=(grp, lax.rem(me + k, n)), device_id_type=MESH)
+        pl.semaphore_signal(barrier, inc=1, device_id=grp + (lax.rem(me + k, n),), device_id_type=MESH)
     pl.semaphore_wait(barrier, n - 1)
     copies = []
     for k in range(1, n):
@@ -140,7 +140,7 @@
             dst_ref=recv.at[k],
             send_sem=send_sem.at[k],
             recv_sem=recv_sem.at[k],
-            device_id=(grp, peer),
+            device_id=grp + (peer,),
             device_id_type=MESH,
         )
         copy.start()
@@ -168,8 +168,8 @@
     )(x)
 
 
-def on_device(n_mem, queries, suffix_kv, prefix_kv, out_weight, node_blocks, root_of, mid_of):
-    group_index = lax.axis_index("grp")
+def on_device(n_mem, n_core, queries, suffix_kv, prefix_kv, out_weight, node_blocks, root_of, mid_of):
+    group_index = lax.axis_index("chip") * n_core + lax.axis_index("core")
     head_index = lax.axis_index("mem")
     tokens_dev, heads_dev, head_dim = queries.shape
     req_local = tokens_dev // SUFFIX
@@ -177,10 +177,14 @@
     kv_start = head_index * heads_dev // group_size
     prefix_part = lax.dynamic_index_in_dim(prefix_kv, kv_start, 3, keepdims=False)
     suffix_part = lax.dynamic_index_in_dim(suffix_kv, kv_start, 2, keepdims=False)
-    kv_all = lax.all_gather(prefix_part, "grp", axis=0, tiled=True)
+    own_blocks = prefix_part.shape[0]
+    kv_half = lax.all_gather(prefix_part, "chip", axis=0, tiled=True)
+    kv_all = lax.all_gather(kv_half, "core", axis=0, tiled=True)
 
     request_ids = group_index * req_local + jnp.arange(req_local)
     ids, counts = path_table(request_ids, node_blocks, root_of, mid_of)
+    owner = ids // own_blocks
+    ids = (owner % n_core) * kv_half.shape[0] + (owner // n_core) * own_blocks + ids % own_blocks
 
     q = queries.reshape(req_local, SUFFIX, heads_dev, head_dim).transpose(0, 2, 1, 3)
     q = q.reshape(req_local, heads_dev * SUFFIX, head_dim)
@@ -198,18 +202,22 @@
 
 
 def solution(mesh):
+    n_core = 2
+    n_grp, n_mem = mesh.shape["grp"], mesh.shape["mem"]
+    fine = Mesh(mesh.devices.reshape(n_grp // n_core, n_core, n_mem), ("chip", "core", "mem"))
+    grp = ("chip", "core")
     return jax.shard_map(
-        functools.partial(on_device, mesh.shape["mem"]),
-        mesh=mesh,
+        functools.partial(on_device, n_mem, n_core),
+        mesh=fine,
         in_specs=(
-            P("grp", "mem", None),
-            P("grp", None, None, None),
-            P("grp", None, None, None, None),
+            P(grp, "mem", None),
+            P(grp, None, None, None),
+            P(grp, None, None, None, None),
             P("mem", None),
             P(),
             P(),
             P(),
         ),
-        out_specs=P(("grp", "mem"), None),
+        out_specs=P(grp + ("mem",), None),
         check_vma=False,
     )

time: 232 us -> 258 us (1.11)
  the two profiles are of different devices: /device:TPU:156 before, /device:TPU:219 now
where the time goes in v2:
time: 258 us
  waiting for transfers between devices  131 us (51%)
  Pallas kernels  98.2 us (38%)
  between operations  13.5 us (5%)
  local copies, waits for them, and re-layouts  9.26 us (4%)
  matrix products  3.65 us (1%)
    all_gather x1, waiting for transfers between devices, on_device(): kv_half = lax.all_gather(prefix_part, 'chip', axis=0, tiled=True)  98.7 us
    pallas_call x1, Pallas kernels, attend(): pl.pallas_call(functools.partial(attend_kernel, slots), out_shape=jax.Sha...  74.5 us
    all_gather x1, waiting for transfers between devices, on_device(): kv_all = lax.all_gather(kv_half, 'core', axis=0, tiled=True)  32.7 us
    pallas_call x1, Pallas kernels, exchange_sum(): pl.pallas_call(functools.partial(exchange_kernel, n), out_shape=jax.Shape...  23.7 us
  transfers between devices with their start and end apart: 2, of which 2 were waited for; matrix products, arithmetic and copies ran while one was open for 2% of the time, Pallas kernels for 0%

profile of v2, /device:TPU:219, one launch (start us, length us, event | category | flops | bytes accessed | tf_op | source)
XLA Modules:
  0.0 257.9 jit_solution(11198032685144552269)
XLA Ops:
  6.5 0.0 copy-start
  6.5 0.0 all-gather.5.cloned.1.call-start
  6.5 3.0 %constant_dynamic-slice_fusion = bf16[8,2,128,1,128]{4,3,2,1,0:T(2,128)(2,1)S(1)} fusion(bf16[8,2,128,4,128]{4,3,2,1,0:T(4,128)(2,1)} %param.9, s32[]{:T(128)S(6)} %select_n.76), kind=kLoop, calls=%fused_computation.36 | loop fusion | bytes 1048580 | tf_op jit(solution)/shard_map/jit(dynamic_index_in_dim)/dynamic_slice | solution.py:178
  9.5 0.9 copy.31
  10.4 0.0 all-gather.5.cloned.1.call-update
  10.4 0.0 all-gather.7.cloned.1.call-start
  10.5 98.7 %all-gather.5.cloned.1.call-done = bf16[128,2,128,1,128]{4,2,3,1,0:T(8,128)(2,1)} async-done(((bf16[8,2,128,1,128]{4,2,3,1,0:T(8,128)(2,1)}), bf16[128,2,128,1,128]{4,2,3,1,0:T(8,128)(2,1)}) %all-gather.5.cloned.1.call-update) | async-done | bytes 8388624 | tf_op jit(solution)/shard_map/all_gather | solution.py:181
  109.2 0.0 copy-start.3
  109.2 0.0 copy-start.4
  109.2 0.0 copy-start.5
  109.2 0.0 all-gather.7.cloned.1.call-update
  109.2 0.0 copy-start.1
  109.3 1.8 constant_dynamic-slice_fusion.1
  111.2 0.0 copy-done.3
  111.2 0.1 copy.25
  111.3 0.1 reduce-window.9
  111.4 0.1 reduce
  111.6 0.0 copy-done.4
  111.6 0.2 fusion
  111.7 0.0 copy-done.5
  111.8 0.2 fusion.1
  112.0 0.3 select_reduce_fusion.2
  112.3 0.0 copy-start.2
  112.3 0.1 fusion.3
  112.3 0.1 select_reduce_fusion.1
  112.4 0.1 compare_select_fusion
  112.5 0.1 select_n.70
  112.6 0.0 copy-done.1
  112.6 0.9 copy.26
  113.5 0.6 fusion.6.ids_ref
  114.1 0.7 fusion.7
  114.8 32.7 %all-gather.7.cloned.1.call-done = bf16[256,2,128,1,128]{4,2,3,1,0:T(8,128)(2,1)} async-done(((bf16[128,2,128,1,128]{4,2,3,1,0:T(8,128)(2,1)}), bf16[256,2,128,1,128]{4,2,3,1,0:T(8,128)(2,1)}) %all-gather.7.cloned.1.call-update) | async-done | bytes 16777232 | tf_op jit(solution)/shard_map/all_gather | solution.py:182
  147.5 0.0 copy-done.2
  147.5 74.5 %shard_map.73 = bf16[2,1024,128]{2,1,0:T(8,128)(2,1)} custom-call(s32[192]{0:T(256)} %fusion.6.ids_ref, s32[2]{0:T(128)} %copy-done.2, bf16[2,1024,128]{2,1,0:T(8,128)(2,1)} %bitcast.32, bf16[2,256,128]{2,1,0:T(8,128)(2,1)} %bitcast.36, bf16[2,256,128]{2,1,0:T(8,128)(2,1)} %bitcast.35, bf16[256,2,128,128]{3,2,1,0:T(8,128)(2,1)} %bitcast.31), custom_call_target="tpu_custom_call" | custom-call | tf_op jit(solution)/shard_map/pallas_call | solution.py:103
  222.0 0.0 copy-done
  222.0 3.7 %bitcast_convert_fusion = bf16[2,256,2048]{2,1,0:T(8,128)(2,1)} fusion(bf16[2,4,256,128]{3,2,1,0:T(8,128)(2,1)} %bitcast.37, bf16[4,128,2048,1]{2,1,0,3:T(8,128)(2,1)S(1)} %bitcast.30), kind=kOutput, calls=%fused_computation | convolution fusion | flops 1074790400 | bytes 4718592 | tf_op jit(solution)/shard_map/dot_general | solution.py:196
  225.6 23.7 %shard_map.74 = bf16[64,2048]{1,0:T(8,128)(2,1)} custom-call(bf16[8,64,2048]{2,1,0:T(8,128)(2,1)} %bitcast.33), custom_call_target="tpu_custom_call" | custom-call | tf_op jit(solution)/shard_map/pallas_call | solution.py:157
  249.3 1.7 copy.35
  (9 shorter events, 0.1 us)
Async XLA Ops:
  6.5 215.4 %copy-start = (bf16[512,2048]{1,0:T(8,128)(2,1)S(1)}, bf16[512,2048]{1,0:T(8,128)(2,1)}, u32[]{:S(2)}) copy-start(bf16[512,2048]{1,0:T(8,128)(2,1)} %param.10) | copy-start | bytes 6291460
  6.5 102.7 %all-gather.5.cloned.1.call-start = ((), (), s32[]{:S(2)}) async-start(), calls=%async_computation | async-start | bytes 8912896 | tf_op jit(solution)/shard_map/all_gather | solution.py:181
  10.4 137.0 %all-gather.7.cloned.1.call-start = ((), (), s32[]{:S(2)}) async-start(), calls=%async_computation.1 | async-start | bytes 25165824 | tf_op jit(solution)/shard_map/all_gather | solution.py:182
  109.2 1.9 copy-start.3
  109.2 2.3 copy-start.4
  109.2 2.5 copy-start.5
  109.2 3.3 %copy-start.1 = (bf16[512,4,128]{2,1,0:T(4,128)(2,1)S(1)}, bf16[512,4,128]{2,1,0:T(4,128)(2,1)}, u32[]{:S(2)}) copy-start(bf16[512,4,128]{2,1,0:T(4,128)(2,1)} %param.7) | copy-start | bytes 1572868
  112.3 35.2 %copy-start.2 = (s32[2]{0:T(128)}, s32[2]{0:T(128)S(1)}, u32[]{:S(2)}) copy-start(s32[2]{0:T(128)S(1)} %get-tuple-element.11.cnt_ref) | copy-start | bytes 28
Sparse Core Ops, SparseCore 0:
  10.5 98.6 all-gather.4
  111.0 36.4 all-gather.6

commit v3 on v1

--- a/solution.py
+++ b/solution.py
@@ -11,6 +11,7 @@
 KVH = 4
 SUFFIX = 256
 MOST_BLK = 32
+N_CHUNK = 4
 NEG = -1e30
 MESH = pl.DeviceIdType.MESH
 
@@ -47,26 +48,68 @@
     return ids.astype(jnp.int32), total.astype(jnp.int32)
 
 
-def attend_kernel(slots, ids_ref, cnt_ref, q_ref, ks_ref, vs_ref, kv_hbm, o_ref, buf, sem, m_sc, l_sc, acc_sc):
-    j = pl.program_id(0)
-    n = cnt_ref[j]
-    rows, hd = q_ref.shape
-    scale = hd ** (-0.5)
+def suffix_kernel(q_ref, ks_ref, vs_ref, m_ref, l_ref, acc_ref):
+    hd = q_ref.shape[-1]
     contract = (((1,), (1,)), ((), ()))
-    q = q_ref[...]
-
-    scores = lax.dot_general(q, ks_ref[...], contract, preferred_element_type=jnp.float32) * scale
+    scores = lax.dot_general(q_ref[...], ks_ref[...], contract, preferred_element_type=jnp.float32)
+    scores = scores * hd ** (-0.5)
     tok = lax.broadcasted_iota(jnp.int32, scores.shape, 0) % SUFFIX
     key = lax.broadcasted_iota(jnp.int32, scores.shape, 1)
     scores = jnp.where(key <= tok, scores, NEG)
     high = jnp.max(scores, axis=-1, keepdims=True)
     weights = jnp.exp(scores - high)
-    m_sc[...] = high
-    l_sc[...] = jnp.sum(weights, axis=-1, keepdims=True)
-    acc_sc[...] = jnp.dot(weights.astype(jnp.bfloat16), vs_ref[...], preferred_element_type=jnp.float32)
+    m_ref[...] = high
+    l_ref[...] = jnp.sum(weights, axis=-1, keepdims=True)
+    acc_ref[...] = jnp.dot(weights.astype(jnp.bfloat16), vs_ref[...], preferred_element_type=jnp.float32)
+
+
+def state_shapes(req, rows, hd):
+    return (
+        jax.ShapeDtypeStruct((req, rows, 1), jnp.float32),
+        jax.ShapeDtypeStruct((req, rows, 1), jnp.float32),
+        jax.ShapeDtypeStruct((req, rows, hd), jnp.float32),
+    )
+
+
+def state_specs(rows, hd, index):
+    return [
+        pl.BlockSpec((None, rows, 1), index),
+        pl.BlockSpec((None, rows, 1), index),
+        pl.BlockSpec((None, rows, hd), index),
+    ]
+
+
+def suffix_part_attend(q, ks, vs):
+    req, rows, hd = q.shape
+    index = lambda j: (j, 0, 0)
+    return pl.pallas_call(
+        suffix_kernel,
+        out_shape=state_shapes(req, rows, hd),
+        grid=(req,),
+        in_specs=[
+            pl.BlockSpec((None, rows, hd), index),
+            pl.BlockSpec((None, SUFFIX, hd), index),
+            pl.BlockSpec((None, SUFFIX, hd), index),
+        ],
+        out_specs=state_specs(rows, hd, index),
+        compiler_params=pltpu.CompilerParams(dimension_semantics=("arbitrary",)),
+    )(q, ks, vs)
+
+
+def chunk_kernel(slots, ids_ref, off_ref, cnt_ref, q_ref, kv_hbm, m_ref, l_ref, acc_ref, buf, sem):
+    j = pl.program_id(0)
+    n = cnt_ref[j]
+    base = j * slots + off_ref[j]
+    hd = q_ref.shape[-1]
+    scale = hd ** (-0.5)
+    contract = (((1,), (1,)), ((), ()))
+    q = q_ref[...]
+    m_ref[...] = jnp.full(m_ref.shape, NEG, jnp.float32)
+    l_ref[...] = jnp.zeros(l_ref.shape, jnp.float32)
+    acc_ref[...] = jnp.zeros(acc_ref.shape, jnp.float32)
 
     def fetch(i, slot):
-        pltpu.make_async_copy(kv_hbm.at[ids_ref[j * slots + i]], buf.at[slot], sem.at[slot]).start()
+        pltpu.make_async_copy(kv_hbm.at[ids_ref[base + i]], buf.at[slot], sem.at[slot]).start()
 
     @pl.when(n > 0)
     def _():
@@ -81,48 +124,43 @@
             fetch(i + 1, 1 - slot)
 
         s = lax.dot_general(q, buf[slot, 0], contract, preferred_element_type=jnp.float32) * scale
-        m_old = m_sc[...]
+        m_old = m_ref[...]
         m_new = jnp.maximum(m_old, jnp.max(s, axis=-1, keepdims=True))
         factor = jnp.exp(m_old - m_new)
         p = jnp.exp(s - m_new)
-        l_sc[...] = l_sc[...] * factor + jnp.sum(p, axis=-1, keepdims=True)
-        acc_sc[...] = acc_sc[...] * factor + jnp.dot(
+        l_ref[...] = l_ref[...] * factor + jnp.sum(p, axis=-1, keepdims=True)
+        acc_ref[...] = acc_ref[...] * factor + jnp.dot(
             p.astype(jnp.bfloat16), buf[slot, 1], preferred_element_type=jnp.float32
         )
-        m_sc[...] = m_new
+        m_ref[...] = m_new
         return carry
 
     lax.fori_loop(0, n, body, 0)
-    o_ref[...] = (acc_sc[...] / l_sc[...]).astype(o_ref.dtype)
-
-
-def attend(ids, counts, q, ks, vs, kv_all):
+
+
+def chunk_attend(ids, offs, cnts, q, kv_chunk):
     req, rows, hd = q.shape
     slots = ids.shape[1]
-    block_shape = kv_all.shape[1:]
+    block_shape = kv_chunk.shape[1:]
+    index = lambda j, ids, off, cnt: (j, 0, 0)
     return pl.pallas_call(
-        functools.partial(attend_kernel, slots),
-        out_shape=jax.ShapeDtypeStruct((req, rows, hd), jnp.bfloat16),
+        functools.partial(chunk_kernel, slots),
+        out_shape=state_shapes(req, rows, hd),
         grid_spec=pltpu.PrefetchScalarGridSpec(
-            num_scalar_prefetch=2,
+            num_scalar_prefetch=3,
             grid=(req,),
             in_specs=[
-                pl.BlockSpec((None, rows, hd), lambda j, ids, cnt: (j, 0, 0)),
-                pl.BlockSpec((None, SUFFIX, hd), lambda j, ids, cnt: (j, 0, 0)),
-                pl.BlockSpec((None, SUFFIX, hd), lambda j, ids, cnt: (j, 0, 0)),
+                pl.BlockSpec((None, rows, hd), index),
                 pl.BlockSpec(memory_space=pl.ANY),
             ],
-            out_specs=pl.BlockSpec((None, rows, hd), lambda j, ids, cnt: (j, 0, 0)),
+            out_specs=state_specs(rows, hd, index),
             scratch_shapes=[
-                pltpu.VMEM((2,) + block_shape, kv_all.dtype),
+                pltpu.VMEM((2,) + block_shape, kv_chunk.dtype),
                 pltpu.SemaphoreType.DMA((2,)),
-                pltpu.VMEM((rows, 1), jnp.float32),
-                pltpu.VMEM((rows, 1), jnp.float32),
-                pltpu.VMEM((rows, hd), jnp.float32),
             ],
         ),
         compiler_params=pltpu.CompilerParams(dimension_semantics=("arbitrary",)),
-    )(ids.reshape(-1), counts, q, ks, vs, kv_all)
+    )(ids.reshape(-1), offs, cnts, q, kv_chunk)
 
 
 def exchange_kernel(n, x_ref, o_ref, recv, send_sem, recv_sem):
@@ -177,16 +215,41 @@
     kv_start = head_index * heads_dev // group_size
     prefix_part = lax.dynamic_index_in_dim(prefix_kv, kv_start, 3, keepdims=False)
     suffix_part = lax.dynamic_index_in_dim(suffix_kv, kv_start, 2, keepdims=False)
-    kv_all = lax.all_gather(prefix_part, "grp", axis=0, tiled=True)
+    own_blocks = prefix_part.shape[0]
+    per_chunk = own_blocks // N_CHUNK
 
     request_ids = group_index * req_local + jnp.arange(req_local)
     ids, counts = path_table(request_ids, node_blocks, root_of, mid_of)
+    slots = jnp.arange(ids.shape[1])[None, :]
+    valid = slots < counts[:, None]
+    chunk_of = (ids % own_blocks) // per_chunk
+    place = (ids // own_blocks) * per_chunk + ids % per_chunk
+    order = jnp.argsort(jnp.where(valid, chunk_of, N_CHUNK) * ids.shape[1] + slots, axis=1)
+    place = jnp.take_along_axis(place, order, axis=1).astype(jnp.int32)
+    chunk_sorted = jnp.take_along_axis(jnp.where(valid, chunk_of, N_CHUNK), order, axis=1)
+    cnts = jnp.sum(chunk_sorted[:, :, None] == jnp.arange(N_CHUNK)[None, None, :], axis=1).astype(jnp.int32)
+    offs = (jnp.cumsum(cnts, axis=1) - cnts).astype(jnp.int32)
 
     q = queries.reshape(req_local, SUFFIX, heads_dev, head_dim).transpose(0, 2, 1, 3)
     q = q.reshape(req_local, heads_dev * SUFFIX, head_dim)
     ks = suffix_part[:, 0].reshape(req_local, SUFFIX, head_dim)
     vs = suffix_part[:, 1].reshape(req_local, SUFFIX, head_dim)
-    attended = attend(ids, counts, q, ks, vs, kv_all)
+    parts = [suffix_part_attend(q, ks, vs)]
+    for c in range(N_CHUNK):
+        kv_chunk = lax.all_gather(
+            prefix_part[c * per_chunk : (c + 1) * per_chunk], "grp", axis=0, tiled=True
+        )
+        parts.append(chunk_attend(place, offs[:, c], cnts[:, c], q, kv_chunk))
+    high = parts[0][0]
+    for m_c, _, _ in parts[1:]:
+        high = jnp.maximum(high, m_c)
+    total = 0.0
+    summed = 0.0
+    for m_c, l_c, acc_c in parts:
+        factor = jnp.exp(m_c - high)
+        total = total + l_c * factor
+        summed = summed + acc_c * factor
+    attended = (summed / total).astype(jnp.bfloat16)
     attended = attended.reshape(req_local, heads_dev, SUFFIX, head_dim)
     w = out_weight.reshape(heads_dev, head_dim, out_weight.shape[1])
     partial = lax.dot_general(

time: 232 us -> 354 us (1.53)
  the two profiles are of different devices: /device:TPU:156 before, /device:TPU:124 now
where the time goes in v3:
time: 354 us; the launch traced here: 348 us
  waiting for transfers between devices  198 us (56%)
  Pallas kernels  106 us (30%)
  local copies, waits for them, and re-layouts  16.7 us (5%)
  between operations  13.4 us (4%)
  other arithmetic  11.3 us (3%)
    all_gather x4, waiting for transfers between devices, on_device(): lax.all_gather(prefix_part[c * per_chunk:(c + 1) * per_chunk], 'grp', axi...  198 us
    pallas_call x4, Pallas kernels, chunk_attend(): pl.pallas_call(functools.partial(chunk_kernel, slots), out_shape=state_sh...  75.8 us
    pallas_call x1, Pallas kernels, exchange_sum(): pl.pallas_call(functools.partial(exchange_kernel, n), out_shape=jax.Shape...  26.7 us
  transfers between devices with their start and end apart: 4, of which 4 were waited for; matrix products, arithmetic and copies ran while one was open for 4% of the time, Pallas kernels for 17%

profile of v3, /device:TPU:124, one launch (start us, length us, event | category | flops | bytes accessed | tf_op | source)
XLA Modules:
  0.0 348.4 jit_solution(2573015327643560492)
XLA Ops:
  6.6 2.8 constant_dynamic-slice_fusion
  9.3 0.7 copy.86
  10.0 0.0 all-gather.15.cloned.1.call-update
  10.0 0.0 all-gather.13.cloned.1.call-start
  10.1 0.7 copy.85
  10.7 0.0 all-gather.13.cloned.1.call-update
  10.8 0.0 all-gather.11.cloned.1.call-start
  10.8 0.7 copy.84
  11.5 0.0 all-gather.9.cloned.1.call-start
  11.6 0.7 copy.83
  12.3 0.1 copy.71
  12.4 0.1 reduce-window.9
  12.5 0.1 reduce
  12.7 0.2 fusion.6
  12.8 0.2 fusion.7
  13.1 0.3 select_reduce_fusion.2
  13.4 0.1 fusion.9
  13.4 0.1 select_reduce_fusion.1
  13.5 0.1 iota_add_fusion
  13.6 0.1 copy.72
  13.7 1.5 sort.17
  15.2 0.1 copy.73
  15.3 0.1 reshape.173
  15.4 2.1 gather_fusion.1
  17.6 0.1 reshape.181
  17.7 2.0 gather_fusion
  19.6 0.1 reshape.176
  19.7 0.7 reshape.142.ids_ref
  20.4 0.1 convert_reduce_fusion
  20.5 0.2 reduce_window_sum.30
  20.7 0.9 copy.69
  21.6 1.8 constant_dynamic-slice_fusion.4
  23.4 0.7 fusion.12
  24.2 3.3 shard_map.73
  27.5 0.8 slice_reduce_fusion.6
  28.3 48.6 %all-gather.15.cloned.1.call-done = bf16[64,2,128,1,128]{4,2,3,1,0:T(8,128)(2,1)} async-done(((bf16[2,2,128,1,128]{4,2,3,1,0:T(8,128)(2,1)}), bf16[64,2,128,1,128]{4,2,3,1,0:T(8,128)(2,1)}) %all-gather.15.cloned.1.call-update) | async-done | bytes 4194320 | tf_op jit(solution)/shard_map/all_gather | solution.py:239
  77.0 22.2 %shard_map.77 = (f32[2,1024,1]{2,1,0:T(8,128)}, f32[2,1024,1]{2,1,0:T(8,128)}, f32[2,1024,128]{2,1,0:T(8,128)}) custom-call(s32[192]{0:T(256)} %reshape.142.ids_ref, s32[2]{0:T(128)} %get-tuple-element.72.off_ref, s32[2]{0:T(128)} %get-tuple-element.47.cnt_ref, bf16[2,1024,128]{2,1,0:T(8,128)(2,1)} %bitcast.40, bf16[64,2,128,128]{3,2,1,0:T(8,128)(2,1)} %bitcast.44), custom_call_target="tpu_custom_call" | custom-call | tf_op jit(solution)/shard_map/pallas_call | solution.py:146
  99.2 46.1 %all-gather.13.cloned.1.call-done = bf16[64,2,128,1,128]{4,2,3,1,0:T(8,128)(2,1)} async-done(((bf16[2,2,128,1,128]{4,2,3,1,0:T(8,128)(2,1)}), bf16[64,2,128,1,128]{4,2,3,1,0:T(8,128)(2,1)}) %all-gather.13.cloned.1.call-update) | async-done | bytes 4194320 | tf_op jit(solution)/shard_map/all_gather | solution.py:239
  145.3 15.4 %shard_map.76 = (f32[2,1024,1]{2,1,0:T(8,128)}, f32[2,1024,1]{2,1,0:T(8,128)}, f32[2,1024,128]{2,1,0:T(8,128)}) custom-call(s32[192]{0:T(256)} %reshape.142.ids_ref, s32[2]{0:T(128)} %get-tuple-element.71.off_ref, s32[2]{0:T(128)} %get-tuple-element.48.cnt_ref, bf16[2,1024,128]{2,1,0:T(8,128)(2,1)} %bitcast.41, bf16[64,2,128,128]{3,2,1,0:T(8,128)(2,1)} %bitcast.45), custom_call_target="tpu_custom_call" | custom-call | tf_op jit(solution)/shard_map/pallas_call | solution.py:146
  160.7 53.0 %all-gather.11.cloned.1.call-done = bf16[64,2,128,1,128]{4,2,3,1,0:T(8,128)(2,1)} async-done(((bf16[2,2,128,1,128]{4,2,3,1,0:T(8,128)(2,1)}), bf16[64,2,128,1,128]{4,2,3,1,0:T(8,128)(2,1)}) %all-gather.11.cloned.1.call-update) | async-done | bytes 4194320 | tf_op jit(solution)/shard_map/all_gather | solution.py:239
  213.7 17.5 %shard_map.75 = (f32[2,1024,1]{2,1,0:T(8,128)}, f32[2,1024,1]{2,1,0:T(8,128)}, f32[2,1024,128]{2,1,0:T(8,128)}) custom-call(s32[192]{0:T(256)} %reshape.142.ids_ref, s32[2]{0:T(128)} %get-tuple-element.70.off_ref, s32[2]{0:T(128)} %get-tuple-element.49.cnt_ref, bf16[2,1024,128]{2,1,0:T(8,128)(2,1)} %bitcast.42, bf16[64,2,128,128]{3,2,1,0:T(8,128)(2,1)} %bitcast.46), custom_call_target="tpu_custom_call" | custom-call | tf_op jit(solution)/shard_map/pallas_call | solution.py:146
  231.2 50.6 %all-gather.9.cloned.1.call-done = bf16[64,2,128,1,128]{4,2,3,1,0:T(8,128)(2,1)} async-done(((bf16[2,2,128,1,128]{4,2,3,1,0:T(8,128)(2,1)}), bf16[64,2,128,1,128]{4,2,3,1,0:T(8,128)(2,1)}) %all-gather.9.cloned.1.call-update) | async-done | bytes 4194320 | tf_op jit(solution)/shard_map/all_gather | solution.py:239
  281.8 20.7 %shard_map.74 = (f32[2,1024,1]{2,1,0:T(8,128)}, f32[2,1024,1]{2,1,0:T(8,128)}, f32[2,1024,128]{2,1,0:T(8,128)}) custom-call(s32[192]{0:T(256)} %reshape.142.ids_ref, s32[2]{0:T(128)} %get-tuple-element.73.off_ref, s32[2]{0:T(128)} %get-tuple-element.46.cnt_ref, bf16[2,1024,128]{2,1,0:T(8,128)(2,1)} %bitcast.43, bf16[64,2,128,128]{3,2,1,0:T(8,128)(2,1)} %bitcast.47), custom_call_target="tpu_custom_call" | custom-call | tf_op jit(solution)/shard_map/pallas_call | solution.py:146
  302.6 6.3 %fusion = (f32[2,1024]{1,0:T(2,128)S(1)}, f32[2,1024]{1,0:T(2,128)S(1)}, f32[2,1024]{1,0:T(2,128)S(1)}, f32[2,1024]{1,0:T(2,128)S(1)}, f32[2,1024]{1,0:T(2,128)S(1)}, /*index=5*/f32[2,1024]{1,0:T(2,128)S(1)}) fusion(f32[2,1024,1]{2,1,0:T(8,128)S(1)} %copy-done.1, f32[2,1024,1]{2,1,0:T(8,128)} %get-tuple-element.37, f32[2,1024,1]{2,1,0:T(8,128)} %get-tuple-element.28, ...), kind=kLoop, calls=%fused_computation.11 | loop fusion | flops 36864 | bytes 131072 | tf_op jit(solution)/shard_map/exp | solution.py:249
  308.9 2.0 divide_convert_fusion
  310.9 2.6 bitcast_convert_fusion
  313.6 26.7 %shard_map.78 = bf16[64,2048]{1,0:T(8,128)(2,1)} custom-call(bf16[8,64,2048]{2,1,0:T(8,128)(2,1)} %bitcast.48), custom_call_target="tpu_custom_call" | custom-call | tf_op jit(solution)/shard_map/pallas_call | solution.py:195
  340.2 1.7 copy.90
  (39 shorter events, 0.2 us)
Async XLA Ops:
  6.5 304.4 %copy-start = (bf16[512,2048]{1,0:T(8,128)(2,1)S(1)}, bf16[512,2048]{1,0:T(8,128)(2,1)}, u32[]{:S(2)}) copy-start(bf16[512,2048]{1,0:T(8,128)(2,1)} %param.12) | copy-start | bytes 6291460
  6.5 70.4 %all-gather.15.cloned.1.call-start = ((), (), s32[]{:S(2)}) async-start(), calls=%async_computation.3 | async-start | bytes 4325376 | tf_op jit(solution)/shard_map/all_gather | solution.py:239
  6.5 5.7 %copy-start.8 = (s32[84]{0:T(128)S(1)}, s32[84]{0:T(128)}, u32[]{:S(2)}) copy-start(s32[84]{0:T(128)} %param.13) | copy-start | bytes 1012
  6.5 6.1 %copy-start.9 = (s32[64]{0:T(128)S(1)}, s32[64]{0:T(128)}, u32[]{:S(2)}) copy-start(s32[64]{0:T(128)} %param.15) | copy-start | bytes 772
  6.5 6.3 %copy-start.10 = (s32[16]{0:T(128)S(1)}, s32[16]{0:T(128)}, u32[]{:S(2)}) copy-start(s32[16]{0:T(128)} %param.14) | copy-start | bytes 196
  10.0 135.3 %all-gather.13.cloned.1.call-start = ((), (), s32[]{:S(2)}) async-start(), calls=%async_computation.2 | async-start | bytes 4325376 | tf_op jit(solution)/shard_map/all_gather | solution.py:239
  10.7 10.0 %copy-start.7 = (bf16[512,4,128]{2,1,0:T(4,128)(2,1)S(1)}, bf16[512,4,128]{2,1,0:T(4,128)(2,1)}, u32[]{:S(2)}) copy-start(bf16[512,4,128]{2,1,0:T(4,128)(2,1)} %param.9) | copy-start | bytes 1572868
  10.8 202.9 %all-gather.11.cloned.1.call-start = ((), (), s32[]{:S(2)}) async-start(), calls=%async_computation.1 | async-start | bytes 4325376 | tf_op jit(solution)/shard_map/all_gather | solution.py:239
  11.5 270.3 %all-gather.9.cloned.1.call-start = ((), (), s32[]{:S(2)}) async-start(), calls=%async_computation | async-start | bytes 4325376 | tf_op jit(solution)/shard_map/all_gather | solution.py:239
  281.8 20.7 %copy-start.1 = (f32[2,1024,1]{2,1,0:T(8,128)S(1)}, f32[2,1024,1]{2,1,0:T(8,128)}, u32[]{:S(2)}) copy-start(f32[2,1024,1]{2,1,0:T(8,128)} %get-tuple-element.23) | copy-start | bytes 24580
  302.5 6.4 %copy-start.2 = (f32[2,1024,128]{2,1,0:T(8,128)S(1)}, f32[2,1024,128]{2,1,0:T(8,128)}, u32[]{:S(2)}) copy-start(f32[2,1024,128]{2,1,0:T(8,128)} %get-tuple-element.22) | copy-start | bytes 3145732
  302.5 6.4 %copy-start.3 = (f32[2,1024,128]{2,1,0:T(8,128)S(1)}, f32[2,1024,128]{2,1,0:T(8,128)}, u32[]{:S(2)}) copy-start(f32[2,1024,128]{2,1,0:T(8,128)} %get-tuple-element.32) | copy-start | bytes 3145732
  302.5 6.4 %copy-start.4 = (f32[2,1024,128]{2,1,0:T(8,128)S(1)}, f32[2,1024,128]{2,1,0:T(8,128)}, u32[]{:S(2)}) copy-start(f32[2,1024,128]{2,1,0:T(8,128)} %get-tuple-element.31) | copy-start | bytes 3145732
  302.5 6.4 %copy-start.5 = (f32[2,1024,128]{2,1,0:T(8,128)S(1)}, f32[2,1024,128]{2,1,0:T(8,128)}, u32[]{:S(2)}) copy-start(f32[2,1024,128]{2,1,0:T(8,128)} %get-tuple-element.30) | copy-start | bytes 3145732
  302.5 6.4 %copy-start.6 = (f32[2,1024,128]{2,1,0:T(8,128)S(1)}, f32[2,1024,128]{2,1,0:T(8,128)}, u32[]{:S(2)}) copy-start(f32[2,1024,128]{2,1,0:T(8,128)} %get-tuple-element.29) | copy-start | bytes 3145732
Sparse Core Ops, SparseCore 0:
  10.1 66.7 all-gather.14
  78.8 66.4 all-gather.12
  147.2 66.4 all-gather.10
  215.4 66.3 all-gather.8

commit v4 on v1

--- a/solution.py
+++ b/solution.py
@@ -11,6 +11,7 @@
 KVH = 4
 SUFFIX = 256
 MOST_BLK = 32
+N_BUF = 4
 NEG = -1e30
 MESH = pl.DeviceIdType.MESH
 
@@ -68,17 +69,20 @@
     def fetch(i, slot):
         pltpu.make_async_copy(kv_hbm.at[ids_ref[j * slots + i]], buf.at[slot], sem.at[slot]).start()
 
-    @pl.when(n > 0)
-    def _():
-        fetch(0, 0)
+    ahead = N_BUF - 1
+    for t in range(ahead):
+
+        @pl.when(t < n)
+        def _():
+            fetch(t, t)
 
     def body(i, carry):
-        slot = i % 2
+        slot = i % N_BUF
         pltpu.make_async_copy(kv_hbm.at[0], buf.at[slot], sem.at[slot]).wait()
 
-        @pl.when(i + 1 < n)
+        @pl.when(i + ahead < n)
         def _():
-            fetch(i + 1, 1 - slot)
+            fetch(i + ahead, (i + ahead) % N_BUF)
 
         s = lax.dot_general(q, buf[slot, 0], contract, preferred_element_type=jnp.float32) * scale
         m_old = m_sc[...]
@@ -114,8 +118,8 @@
             ],
             out_specs=pl.BlockSpec((None, rows, hd), lambda j, ids, cnt: (j, 0, 0)),
             scratch_shapes=[
-                pltpu.VMEM((2,) + block_shape, kv_all.dtype),
-                pltpu.SemaphoreType.DMA((2,)),
+                pltpu.VMEM((N_BUF,) + block_shape, kv_all.dtype),
+                pltpu.SemaphoreType.DMA((N_BUF,)),
                 pltpu.VMEM((rows, 1), jnp.float32),
                 pltpu.VMEM((rows, 1), jnp.float32),
                 pltpu.VMEM((rows, hd), jnp.float32),

time: 232 us -> 221 us (0.953)
  the two profiles are of different devices: /device:TPU:156 before, /device:TPU:92 now
where the time goes in v4:
time: 221 us
  waiting for transfers between devices  96.4 us (44%)
  Pallas kernels  96.3 us (44%)
  between operations  13.5 us (6%)
  local copies, waits for them, and re-layouts  9.74 us (4%)
  matrix products  3.65 us (2%)
    all_gather x1, waiting for transfers between devices, on_device(): kv_all = lax.all_gather(prefix_part, 'grp', axis=0, tiled=True)  96.4 us
    pallas_call x1, Pallas kernels, attend(): pl.pallas_call(functools.partial(attend_kernel, slots), out_shape=jax.Sha...  71.5 us
    pallas_call x1, Pallas kernels, exchange_sum(): pl.pallas_call(functools.partial(exchange_kernel, n), out_shape=jax.Shape...  24.9 us
  transfers between devices with their start and end apart: 1, of which 1 were waited for; matrix products, arithmetic and copies ran while one was open for 2% of the time, Pallas kernels for 0%

profile of v4, /device:TPU:92, one launch (start us, length us, event | category | flops | bytes accessed | tf_op | source)
XLA Modules:
  0.0 220.9 jit_solution(18018363120755466716)
XLA Ops:
  6.5 0.0 copy-start
  6.5 0.0 all-gather.3.cloned.1.call-start
  6.5 3.0 %constant_dynamic-slice_fusion = bf16[8,2,128,1,128]{4,3,2,1,0:T(2,128)(2,1)S(1)} fusion(bf16[8,2,128,4,128]{4,3,2,1,0:T(4,128)(2,1)} %param.9, s32[]{:T(128)S(6)} %select_n.50), kind=kLoop, calls=%fused_computation.23 | loop fusion | bytes 1048580 | tf_op jit(solution)/shard_map/jit(dynamic_index_in_dim)/dynamic_slice | solution.py:182
  9.5 0.0 copy-start.3
  9.5 0.0 copy-start.4
  9.5 0.0 copy-start.5
  9.5 0.0 copy-start.1
  9.6 0.9 copy.31
  10.5 0.0 all-gather.3.cloned.1.call-update
  10.5 1.8 constant_dynamic-slice_fusion.1
  12.3 0.0 copy-done.3
  12.3 0.1 copy.25
  12.4 0.1 reduce-window.9
  12.6 0.1 reduce
  12.7 0.0 copy-done.4
  12.7 0.2 fusion
  12.9 0.0 copy-done.5
  12.9 0.2 fusion.1
  13.1 0.3 select_reduce_fusion.2
  13.4 0.0 copy-start.2
  13.4 0.1 fusion.3
  13.5 0.1 select_reduce_fusion.1
  13.6 0.1 compare_select_fusion
  13.7 0.7 select_n.48.ids_ref
  14.3 0.0 copy-done.1
  14.3 0.9 copy.26
  15.2 0.7 fusion.4
  15.9 96.4 %all-gather.3.cloned.1.call-done = bf16[256,2,128,1,128]{4,2,3,1,0:T(8,128)(2,1)} async-done(((bf16[8,2,128,1,128]{4,2,3,1,0:T(8,128)(2,1)}), bf16[256,2,128,1,128]{4,2,3,1,0:T(8,128)(2,1)}) %all-gather.3.cloned.1.call-update) | async-done | bytes 16777232 | tf_op jit(solution)/shard_map/all_gather | solution.py:184
  112.3 0.0 copy-done.2
  112.3 71.5 %shard_map.73 = bf16[2,1024,128]{2,1,0:T(8,128)(2,1)} custom-call(s32[192]{0:T(256)} %select_n.48.ids_ref, s32[2]{0:T(128)} %copy-done.2, bf16[2,1024,128]{2,1,0:T(8,128)(2,1)} %bitcast.32, bf16[2,256,128]{2,1,0:T(8,128)(2,1)} %bitcast.36, bf16[2,256,128]{2,1,0:T(8,128)(2,1)} %bitcast.35, bf16[256,2,128,128]{3,2,1,0:T(8,128)(2,1)} %bitcast.31), custom_call_target="tpu_custom_call" | custom-call | tf_op jit(solution)/shard_map/pallas_call | solution.py:107
  183.8 0.0 copy-done
  183.8 3.7 %bitcast_convert_fusion = bf16[2,256,2048]{2,1,0:T(8,128)(2,1)} fusion(bf16[2,4,256,128]{3,2,1,0:T(8,128)(2,1)} %bitcast.37, bf16[4,128,2048,1]{2,1,0,3:T(8,128)(2,1)S(1)} %bitcast.30), kind=kOutput, calls=%fused_computation | convolution fusion | flops 1074790400 | bytes 4718592 | tf_op jit(solution)/shard_map/dot_general | solution.py:196
  187.5 24.9 %shard_map.74 = bf16[64,2048]{1,0:T(8,128)(2,1)} custom-call(bf16[8,64,2048]{2,1,0:T(8,128)(2,1)} %bitcast.33), custom_call_target="tpu_custom_call" | custom-call | tf_op jit(solution)/shard_map/pallas_call | solution.py:161
  212.3 1.7 copy.35
  (9 shorter events, 0.1 us)
Async XLA Ops:
  6.5 177.3 %copy-start = (bf16[512,2048]{1,0:T(8,128)(2,1)S(1)}, bf16[512,2048]{1,0:T(8,128)(2,1)}, u32[]{:S(2)}) copy-start(bf16[512,2048]{1,0:T(8,128)(2,1)} %param.10) | copy-start | bytes 6291460
  6.5 105.8 %all-gather.3.cloned.1.call-start = ((), (), s32[]{:S(2)}) async-start(), calls=%async_computation | async-start | bytes 17301504 | tf_op jit(solution)/shard_map/all_gather | solution.py:184
  9.5 2.8 %copy-start.3 = (s32[84]{0:T(128)S(1)}, s32[84]{0:T(128)}, u32[]{:S(2)}) copy-start(s32[84]{0:T(128)} %param.11) | copy-start | bytes 1012
  9.5 3.2 %copy-start.4 = (s32[64]{0:T(128)S(1)}, s32[64]{0:T(128)}, u32[]{:S(2)}) copy-start(s32[64]{0:T(128)} %param.13) | copy-start | bytes 772
  9.5 3.4 %copy-start.5 = (s32[16]{0:T(128)S(1)}, s32[16]{0:T(128)}, u32[]{:S(2)}) copy-start(s32[16]{0:T(128)} %param.12) | copy-start | bytes 196
  9.5 4.8 %copy-start.1 = (bf16[512,4,128]{2,1,0:T(4,128)(2,1)S(1)}, bf16[512,4,128]{2,1,0:T(4,128)(2,1)}, u32[]{:S(2)}) copy-start(bf16[512,4,128]{2,1,0:T(4,128)(2,1)} %param.7) | copy-start | bytes 1572868
  13.4 98.9 %copy-start.2 = (s32[2]{0:T(128)}, s32[2]{0:T(128)S(1)}, u32[]{:S(2)}) copy-start(s32[2]{0:T(128)S(1)} %get-tuple-element.11.cnt_ref) | copy-start | bytes 28
Sparse Core Ops, SparseCore 0:
  10.6 101.6 all-gather.2

commit v5 on v1

--- a/solution.py
+++ b/solution.py
@@ -11,6 +11,7 @@
 KVH = 4
 SUFFIX = 256
 MOST_BLK = 32
+GROUP = 4
 NEG = -1e30
 MESH = pl.DeviceIdType.MESH
 
@@ -47,7 +48,7 @@
     return ids.astype(jnp.int32), total.astype(jnp.int32)
 
 
-def attend_kernel(slots, ids_ref, cnt_ref, q_ref, ks_ref, vs_ref, kv_hbm, o_ref, buf, sem, m_sc, l_sc, acc_sc):
+def attend_kernel(slots, ids_ref, cnt_ref, q_ref, ks_ref, vs_ref, kv_hbm, o_ref, kbuf, vbuf, sem, m_sc, l_sc, acc_sc):
     j = pl.program_id(0)
     n = cnt_ref[j]
     rows, hd = q_ref.shape
@@ -65,34 +66,51 @@
     l_sc[...] = jnp.sum(weights, axis=-1, keepdims=True)
     acc_sc[...] = jnp.dot(weights.astype(jnp.bfloat16), vs_ref[...], preferred_element_type=jnp.float32)
 
-    def fetch(i, slot):
-        pltpu.make_async_copy(kv_hbm.at[ids_ref[j * slots + i]], buf.at[slot], sem.at[slot]).start()
-
-    @pl.when(n > 0)
+    rows_blk = kbuf.shape[1] // GROUP
+    steps = (n + GROUP - 1) // GROUP
+
+    def copies(step, slot, fresh):
+        for g in range(GROUP):
+            bid = ids_ref[j * slots + step * GROUP + g] if fresh else 0
+            for half, dst in ((0, kbuf), (1, vbuf)):
+                yield pltpu.make_async_copy(
+                    kv_hbm.at[bid, half],
+                    dst.at[slot, pl.ds(g * rows_blk, rows_blk)],
+                    sem.at[slot, g, half],
+                )
+
+    def fetch(step, slot):
+        for c in copies(step, slot, True):
+            c.start()
+
+    @pl.when(steps > 0)
     def _():
         fetch(0, 0)
 
-    def body(i, carry):
-        slot = i % 2
-        pltpu.make_async_copy(kv_hbm.at[0], buf.at[slot], sem.at[slot]).wait()
-
-        @pl.when(i + 1 < n)
+    def body(st, carry):
+        slot = st % 2
+        for c in copies(st, slot, False):
+            c.wait()
+
+        @pl.when(st + 1 < steps)
         def _():
-            fetch(i + 1, 1 - slot)
-
-        s = lax.dot_general(q, buf[slot, 0], contract, preferred_element_type=jnp.float32) * scale
+            fetch(st + 1, 1 - slot)
+
+        s = lax.dot_general(q, kbuf[slot], contract, preferred_element_type=jnp.float32) * scale
+        col = lax.broadcasted_iota(jnp.int32, s.shape, 1)
+        s = jnp.where(col < (n - st * GROUP) * rows_blk, s, NEG)
         m_old = m_sc[...]
         m_new = jnp.maximum(m_old, jnp.max(s, axis=-1, keepdims=True))
         factor = jnp.exp(m_old - m_new)
         p = jnp.exp(s - m_new)
         l_sc[...] = l_sc[...] * factor + jnp.sum(p, axis=-1, keepdims=True)
         acc_sc[...] = acc_sc[...] * factor + jnp.dot(
-            p.astype(jnp.bfloat16), buf[slot, 1], preferred_element_type=jnp.float32
+            p.astype(jnp.bfloat16), vbuf[slot], preferred_element_type=jnp.float32
         )
         m_sc[...] = m_new
         return carry
 
-    lax.fori_loop(0, n, body, 0)
+    lax.fori_loop(0, steps, body, 0)
     o_ref[...] = (acc_sc[...] / l_sc[...]).astype(o_ref.dtype)
 
 
@@ -114,8 +132,9 @@
             ],
             out_specs=pl.BlockSpec((None, rows, hd), lambda j, ids, cnt: (j, 0, 0)),
             scratch_shapes=[
-                pltpu.VMEM((2,) + block_shape, kv_all.dtype),
-                pltpu.SemaphoreType.DMA((2,)),
+                pltpu.VMEM((2, GROUP * block_shape[1], block_shape[2]), kv_all.dtype),
+                pltpu.VMEM((2, GROUP * block_shape[1], block_shape[2]), kv_all.dtype),
+                pltpu.SemaphoreType.DMA((2, GROUP, 2)),
                 pltpu.VMEM((rows, 1), jnp.float32),
                 pltpu.VMEM((rows, 1), jnp.float32),
                 pltpu.VMEM((rows, hd), jnp.float32),

time: 232 us -> 194 us (0.84)
  the two profiles are of different devices: /device:TPU:156 before, /device:TPU:124 now
where the time goes in v5:
time: 194 us
  waiting for transfers between devices  97.3 us (50%)
  Pallas kernels  68.4 us (35%)
  between operations  13.5 us (7%)
  local copies, waits for them, and re-layouts  9.74 us (5%)
  matrix products  3.65 us (2%)
    all_gather x1, waiting for transfers between devices, on_device(): kv_all = lax.all_gather(prefix_part, 'grp', axis=0, tiled=True)  97.3 us
    pallas_call x1, Pallas kernels, attend(): pl.pallas_call(functools.partial(attend_kernel, slots), out_shape=jax.Sha...  43.5 us
    pallas_call x1, Pallas kernels, exchange_sum(): pl.pallas_call(functools.partial(exchange_kernel, n), out_shape=jax.Shape...  24.9 us
  transfers between devices with their start and end apart: 1, of which 1 were waited for; matrix products, arithmetic and copies ran while one was open for 3% of the time, Pallas kernels for 0%

profile of v5, /device:TPU:124, one launch (start us, length us, event | category | flops | bytes accessed | tf_op | source)
XLA Modules:
  0.0 193.8 jit_solution(4216959831403172516)
XLA Ops:
  6.5 0.0 copy-start
  6.5 0.0 all-gather.3.cloned.1.call-start
  6.5 3.0 %constant_dynamic-slice_fusion = bf16[8,2,128,1,128]{4,3,2,1,0:T(2,128)(2,1)S(1)} fusion(bf16[8,2,128,4,128]{4,3,2,1,0:T(4,128)(2,1)} %param.9, s32[]{:T(128)S(6)} %select_n.50), kind=kLoop, calls=%fused_computation.23 | loop fusion | bytes 1048580 | tf_op jit(solution)/shard_map/jit(dynamic_index_in_dim)/dynamic_slice | solution.py:197
  9.5 0.0 copy-start.3
  9.5 0.0 copy-start.4
  9.5 0.0 copy-start.5
  9.5 0.0 copy-start.1
  9.6 0.9 copy.31
  10.5 0.0 all-gather.3.cloned.1.call-update
  10.5 1.8 constant_dynamic-slice_fusion.1
  12.3 0.0 copy-done.3
  12.3 0.1 copy.25
  12.4 0.1 reduce-window.9
  12.6 0.1 reduce
  12.7 0.0 copy-done.4
  12.7 0.2 fusion
  12.9 0.0 copy-done.5
  12.9 0.2 fusion.1
  13.1 0.3 select_reduce_fusion.2
  13.4 0.0 copy-start.2
  13.4 0.1 fusion.3
  13.5 0.1 select_reduce_fusion.1
  13.6 0.1 compare_select_fusion
  13.7 0.7 select_n.48.ids_ref
  14.3 0.0 copy-done.1
  14.3 0.9 copy.26
  15.2 0.7 fusion.4
  15.9 97.3 %all-gather.3.cloned.1.call-done = bf16[256,2,128,1,128]{4,2,3,1,0:T(8,128)(2,1)} async-done(((bf16[8,2,128,1,128]{4,2,3,1,0:T(8,128)(2,1)}), bf16[256,2,128,1,128]{4,2,3,1,0:T(8,128)(2,1)}) %all-gather.3.cloned.1.call-update) | async-done | bytes 16777232 | tf_op jit(solution)/shard_map/all_gather | solution.py:199
  113.2 0.0 copy-done.2
  113.2 43.5 %shard_map.73 = bf16[2,1024,128]{2,1,0:T(8,128)(2,1)} custom-call(s32[192]{0:T(256)} %select_n.48.ids_ref, s32[2]{0:T(128)} %copy-done.2, bf16[2,1024,128]{2,1,0:T(8,128)(2,1)} %bitcast.32, bf16[2,256,128]{2,1,0:T(8,128)(2,1)} %bitcast.36, bf16[2,256,128]{2,1,0:T(8,128)(2,1)} %bitcast.35, bf16[256,2,128,128]{3,2,1,0:T(8,128)(2,1)} %bitcast.31), custom_call_target="tpu_custom_call" | custom-call | tf_op jit(solution)/shard_map/pallas_call | solution.py:121
  156.7 0.0 copy-done
  156.7 3.7 %bitcast_convert_fusion = bf16[2,256,2048]{2,1,0:T(8,128)(2,1)} fusion(bf16[2,4,256,128]{3,2,1,0:T(8,128)(2,1)} %bitcast.37, bf16[4,128,2048,1]{2,1,0,3:T(8,128)(2,1)S(1)} %bitcast.30), kind=kOutput, calls=%fused_computation | convolution fusion | flops 1074790400 | bytes 4718592 | tf_op jit(solution)/shard_map/dot_general | solution.py:211
  160.4 24.9 %shard_map.74 = bf16[64,2048]{1,0:T(8,128)(2,1)} custom-call(bf16[8,64,2048]{2,1,0:T(8,128)(2,1)} %bitcast.33), custom_call_target="tpu_custom_call" | custom-call | tf_op jit(solution)/shard_map/pallas_call | solution.py:176
  185.2 1.7 copy.35
  (9 shorter events, 0.1 us)
Async XLA Ops:
  6.5 150.2 %copy-start = (bf16[512,2048]{1,0:T(8,128)(2,1)S(1)}, bf16[512,2048]{1,0:T(8,128)(2,1)}, u32[]{:S(2)}) copy-start(bf16[512,2048]{1,0:T(8,128)(2,1)} %param.10) | copy-start | bytes 6291460
  6.5 106.6 %all-gather.3.cloned.1.call-start = ((), (), s32[]{:S(2)}) async-start(), calls=%async_computation | async-start | bytes 17301504 | tf_op jit(solution)/shard_map/all_gather | solution.py:199
  9.5 2.8 %copy-start.3 = (s32[84]{0:T(128)S(1)}, s32[84]{0:T(128)}, u32[]{:S(2)}) copy-start(s32[84]{0:T(128)} %param.11) | copy-start | bytes 1012
  9.5 3.2 %copy-start.4 = (s32[64]{0:T(128)S(1)}, s32[64]{0:T(128)}, u32[]{:S(2)}) copy-start(s32[64]{0:T(128)} %param.13) | copy-start | bytes 772
  9.5 3.4 %copy-start.5 = (s32[16]{0:T(128)S(1)}, s32[16]{0:T(128)}, u32[]{:S(2)}) copy-start(s32[16]{0:T(128)} %param.12) | copy-start | bytes 196
  9.5 4.8 %copy-start.1 = (bf16[512,4,128]{2,1,0:T(4,128)(2,1)S(1)}, bf16[512,4,128]{2,1,0:T(4,128)(2,1)}, u32[]{:S(2)}) copy-start(bf16[512,4,128]{2,1,0:T(4,128)(2,1)} %param.7) | copy-start | bytes 1572868
  13.4 99.7 %copy-start.2 = (s32[2]{0:T(128)}, s32[2]{0:T(128)S(1)}, u32[]{:S(2)}) copy-start(s32[2]{0:T(128)S(1)} %get-tuple-element.11.cnt_ref) | copy-start | bytes 28
Sparse Core Ops, SparseCore 0:
  10.6 102.5 all-gather.2

commit v6 on v5

--- a/solution.py
+++ b/solution.py
@@ -11,7 +11,7 @@
 KVH = 4
 SUFFIX = 256
 MOST_BLK = 32
-GROUP = 4
+GROUP = 8
 NEG = -1e30
 MESH = pl.DeviceIdType.MESH
 
@@ -96,18 +96,31 @@
         def _():
             fetch(st + 1, 1 - slot)
 
-        s = lax.dot_general(q, kbuf[slot], contract, preferred_element_type=jnp.float32) * scale
-        col = lax.broadcasted_iota(jnp.int32, s.shape, 1)
-        s = jnp.where(col < (n - st * GROUP) * rows_blk, s, NEG)
-        m_old = m_sc[...]
-        m_new = jnp.maximum(m_old, jnp.max(s, axis=-1, keepdims=True))
-        factor = jnp.exp(m_old - m_new)
-        p = jnp.exp(s - m_new)
-        l_sc[...] = l_sc[...] * factor + jnp.sum(p, axis=-1, keepdims=True)
-        acc_sc[...] = acc_sc[...] * factor + jnp.dot(
-            p.astype(jnp.bfloat16), vbuf[slot], preferred_element_type=jnp.float32
-        )
-        m_sc[...] = m_new
+        limit = (n - st * GROUP) * rows_blk
+
+        def update(masked):
+            s = lax.dot_general(q, kbuf[slot], contract, preferred_element_type=jnp.float32) * scale
+            if masked:
+                col = lax.broadcasted_iota(jnp.int32, s.shape, 1)
+                s = jnp.where(col < limit, s, NEG)
+            m_old = m_sc[...]
+            m_new = jnp.maximum(m_old, jnp.max(s, axis=-1, keepdims=True))
+            factor = jnp.exp(m_old - m_new)
+            p = jnp.exp(s - m_new)
+            l_sc[...] = l_sc[...] * factor + jnp.sum(p, axis=-1, keepdims=True)
+            acc_sc[...] = acc_sc[...] * factor + jnp.dot(
+                p.astype(jnp.bfloat16), vbuf[slot], preferred_element_type=jnp.float32
+            )
+            m_sc[...] = m_new
+
+        @pl.when(limit >= kbuf.shape[1])
+        def _():
+            update(False)
+
+        @pl.when(limit < kbuf.shape[1])
+        def _():
+            update(True)
+
         return carry
 
     lax.fori_loop(0, steps, body, 0)

time: 194 us -> 179 us (0.923)
  the two profiles are of different devices: /device:TPU:124 before, /device:TPU:250 now
where the time goes in v6:
time: 179 us
  waiting for transfers between devices  94.5 us (53%)
  Pallas kernels  56 us (31%)
  between operations  13.5 us (8%)
  local copies, waits for them, and re-layouts  9.74 us (5%)
  matrix products  3.65 us (2%)
    all_gather x1, waiting for transfers between devices, on_device(): kv_all = lax.all_gather(prefix_part, 'grp', axis=0, tiled=True)  94.4 us
    pallas_call x1, Pallas kernels, exchange_sum(): pl.pallas_call(functools.partial(exchange_kernel, n), out_shape=jax.Shape...  39.6 us
    pallas_call x1, Pallas kernels, attend(): pl.pallas_call(functools.partial(attend_kernel, slots), out_shape=jax.Sha...  16.4 us
    dot_general x1, matrix products, on_device(): lax.dot_general(attended, w, (((1, 3), (0, 1)), ((), ())), preferred_elem...  3.65 us
  transfers between devices with their start and end apart: 1, of which 1 were waited for; matrix products, arithmetic and copies ran while one was open for 3% of the time, Pallas kernels for 0%

profile of v6, /device:TPU:250, one launch (start us, length us, event | category | flops | bytes accessed | tf_op | source)
XLA Modules:
  0.0 178.5 jit_solution(16914352812293404002)
XLA Ops:
  6.5 0.0 copy-start
  6.5 0.0 all-gather.3.cloned.1.call-start
  6.5 3.0 %constant_dynamic-slice_fusion = bf16[8,2,128,1,128]{4,3,2,1,0:T(2,128)(2,1)S(1)} fusion(bf16[8,2,128,4,128]{4,3,2,1,0:T(4,128)(2,1)} %param.9, s32[]{:T(128)S(6)} %select_n.50), kind=kLoop, calls=%fused_computation.23 | loop fusion | bytes 1048580 | tf_op jit(solution)/shard_map/jit(dynamic_index_in_dim)/dynamic_slice | solution.py:210
  9.5 0.0 copy-start.3
  9.5 0.0 copy-start.4
  9.5 0.0 copy-start.5
  9.5 0.0 copy-start.1
  9.6 0.9 copy.31
  10.5 0.0 all-gather.3.cloned.1.call-update
  10.5 1.8 constant_dynamic-slice_fusion.1
  12.3 0.0 copy-done.3
  12.3 0.1 copy.25
  12.4 0.1 reduce-window.9
  12.6 0.1 reduce
  12.7 0.0 copy-done.4
  12.7 0.2 fusion
  12.9 0.0 copy-done.5
  12.9 0.2 fusion.1
  13.1 0.3 select_reduce_fusion.2
  13.4 0.0 copy-start.2
  13.4 0.1 fusion.3
  13.5 0.1 select_reduce_fusion.1
  13.6 0.1 compare_select_fusion
  13.7 0.7 select_n.48.ids_ref
  14.3 0.0 copy-done.1
  14.3 0.9 copy.26
  15.2 0.7 fusion.4
  15.9 94.4 %all-gather.3.cloned.1.call-done = bf16[256,2,128,1,128]{4,2,3,1,0:T(8,128)(2,1)} async-done(((bf16[8,2,128,1,128]{4,2,3,1,0:T(8,128)(2,1)}), bf16[256,2,128,1,128]{4,2,3,1,0:T(8,128)(2,1)}) %all-gather.3.cloned.1.call-update) | async-done | bytes 16777232 | tf_op jit(solution)/shard_map/all_gather | solution.py:212
  110.3 0.0 copy-done.2
  110.3 16.4 %shard_map.73 = bf16[2,1024,128]{2,1,0:T(8,128)(2,1)} custom-call(s32[192]{0:T(256)} %select_n.48.ids_ref, s32[2]{0:T(128)} %copy-done.2, bf16[2,1024,128]{2,1,0:T(8,128)(2,1)} %bitcast.32, bf16[2,256,128]{2,1,0:T(8,128)(2,1)} %bitcast.36, bf16[2,256,128]{2,1,0:T(8,128)(2,1)} %bitcast.35, bf16[256,2,128,128]{3,2,1,0:T(8,128)(2,1)} %bitcast.31), custom_call_target="tpu_custom_call" | custom-call | tf_op jit(solution)/shard_map/pallas_call | solution.py:134
  126.7 0.0 copy-done
  126.7 3.7 %bitcast_convert_fusion = bf16[2,256,2048]{2,1,0:T(8,128)(2,1)} fusion(bf16[2,4,256,128]{3,2,1,0:T(8,128)(2,1)} %bitcast.37, bf16[4,128,2048,1]{2,1,0,3:T(8,128)(2,1)S(1)} %bitcast.30), kind=kOutput, calls=%fused_computation | convolution fusion | flops 1074790400 | bytes 4718592 | tf_op jit(solution)/shard_map/dot_general | solution.py:224
  130.4 39.6 %shard_map.74 = bf16[64,2048]{1,0:T(8,128)(2,1)} custom-call(bf16[8,64,2048]{2,1,0:T(8,128)(2,1)} %bitcast.33), custom_call_target="tpu_custom_call" | custom-call | tf_op jit(solution)/shard_map/pallas_call | solution.py:189
  170.0 1.7 copy.35
  (9 shorter events, 0.1 us)
Async XLA Ops:
  6.5 120.2 %copy-start = (bf16[512,2048]{1,0:T(8,128)(2,1)S(1)}, bf16[512,2048]{1,0:T(8,128)(2,1)}, u32[]{:S(2)}) copy-start(bf16[512,2048]{1,0:T(8,128)(2,1)} %param.10) | copy-start | bytes 6291460
  6.5 103.8 %all-gather.3.cloned.1.call-start = ((), (), s32[]{:S(2)}) async-start(), calls=%async_computation | async-start | bytes 17301504 | tf_op jit(solution)/shard_map/all_gather | solution.py:212
  9.5 2.8 %copy-start.3 = (s32[84]{0:T(128)S(1)}, s32[84]{0:T(128)}, u32[]{:S(2)}) copy-start(s32[84]{0:T(128)} %param.11) | copy-start | bytes 1012
  9.5 3.2 %copy-start.4 = (s32[64]{0:T(128)S(1)}, s32[64]{0:T(128)}, u32[]{:S(2)}) copy-start(s32[64]{0:T(128)} %param.13) | copy-start | bytes 772
  9.5 3.4 %copy-start.5 = (s32[16]{0:T(128)S(1)}, s32[16]{0:T(128)}, u32[]{:S(2)}) copy-start(s32[16]{0:T(128)} %param.12) | copy-start | bytes 196
  9.5 4.8 %copy-start.1 = (bf16[512,4,128]{2,1,0:T(4,128)(2,1)S(1)}, bf16[512,4,128]{2,1,0:T(4,128)(2,1)}, u32[]{:S(2)}) copy-start(bf16[512,4,128]{2,1,0:T(4,128)(2,1)} %param.7) | copy-start | bytes 1572868
  13.4 96.9 %copy-start.2 = (s32[2]{0:T(128)}, s32[2]{0:T(128)S(1)}, u32[]{:S(2)}) copy-start(s32[2]{0:T(128)S(1)} %get-tuple-element.11.cnt_ref) | copy-start | bytes 28
Sparse Core Ops, SparseCore 0:
  10.6 99.6 all-gather.2

commit v7 on v6

--- a/solution.py
+++ b/solution.py
@@ -5,7 +5,7 @@
 from jax import lax
 from jax.experimental import pallas as pl
 from jax.experimental.pallas import tpu as pltpu
-from jax.sharding import PartitionSpec as P
+from jax.sharding import Mesh, PartitionSpec as P
 
 QH = 32
 KVH = 4
@@ -159,10 +159,10 @@
 
 def exchange_kernel(n, x_ref, o_ref, recv, send_sem, recv_sem):
     me = lax.axis_index("mem")
-    grp = lax.axis_index("grp")
+    grp = (lax.axis_index("xl"), lax.axis_index("zc"))
     barrier = pltpu.get_barrier_semaphore()
     for k in range(1, n):
-        pl.semaphore_signal(barrier, inc=1, device_id=(grp, lax.rem(me + k, n)), device_id_type=MESH)
+        pl.semaphore_signal(barrier, inc=1, device_id=grp + (lax.rem(me + k, n),), device_id_type=MESH)
     pl.semaphore_wait(barrier, n - 1)
     copies = []
     for k in range(1, n):
@@ -172,7 +172,7 @@
             dst_ref=recv.at[k],
             send_sem=send_sem.at[k],
             recv_sem=recv_sem.at[k],
-            device_id=(grp, peer),
+            device_id=grp + (peer,),
             device_id_type=MESH,
         )
         copy.start()
@@ -200,8 +200,8 @@
     )(x)
 
 
-def on_device(n_mem, queries, suffix_kv, prefix_kv, out_weight, node_blocks, root_of, mid_of):
-    group_index = lax.axis_index("grp")
+def on_device(n_mem, n_zc, queries, suffix_kv, prefix_kv, out_weight, node_blocks, root_of, mid_of):
+    group_index = lax.axis_index("xl") * n_zc + lax.axis_index("zc")
     head_index = lax.axis_index("mem")
     tokens_dev, heads_dev, head_dim = queries.shape
     req_local = tokens_dev // SUFFIX
@@ -209,10 +209,14 @@
     kv_start = head_index * heads_dev // group_size
     prefix_part = lax.dynamic_index_in_dim(prefix_kv, kv_start, 3, keepdims=False)
     suffix_part = lax.dynamic_index_in_dim(suffix_kv, kv_start, 2, keepdims=False)
-    kv_all = lax.all_gather(prefix_part, "grp", axis=0, tiled=True)
+    own_blocks = prefix_part.shape[0]
+    kv_pair = lax.all_gather(prefix_part, "xl", axis=0, tiled=True)
+    kv_all = lax.all_gather(kv_pair, "zc", axis=0, tiled=True)
 
     request_ids = group_index * req_local + jnp.arange(req_local)
     ids, counts = path_table(request_ids, node_blocks, root_of, mid_of)
+    owner = ids // own_blocks
+    ids = (owner % n_zc) * kv_pair.shape[0] + (owner // n_zc) * own_blocks + ids % own_blocks
 
     q = queries.reshape(req_local, SUFFIX, heads_dev, head_dim).transpose(0, 2, 1, 3)
     q = q.reshape(req_local, heads_dev * SUFFIX, head_dim)
@@ -230,18 +234,22 @@
 
 
 def solution(mesh):
+    n_xl = 2
+    n_grp, n_mem = mesh.shape["grp"], mesh.shape["mem"]
+    fine = Mesh(mesh.devices.reshape(n_xl, n_grp // n_xl, n_mem), ("xl", "zc", "mem"))
+    grp = ("xl", "zc")
     return jax.shard_map(
-        functools.partial(on_device, mesh.shape["mem"]),
-        mesh=mesh,
+        functools.partial(on_device, n_mem, n_grp // n_xl),
+        mesh=fine,
         in_specs=(
-            P("grp", "mem", None),
-            P("grp", None, None, None),
-            P("grp", None, None, None, None),
+            P(grp, "mem", None),
+            P(grp, None, None, None),
+            P(grp, None, None, None, None),
             P("mem", None),
             P(),
             P(),
             P(),
         ),
-        out_specs=P(("grp", "mem"), None),
+        out_specs=P(grp + ("mem",), None),
         check_vma=False,
     )

time: 179 us -> 202 us (1.13)
  the two profiles are of different devices: /device:TPU:250 before, /device:TPU:124 now
where the time goes in v7:
time: 202 us
  waiting for transfers between devices  120 us (59%)
  Pallas kernels  53.2 us (26%)
  between operations  13.5 us (7%)
  local copies, waits for them, and re-layouts  9.15 us (5%)
  matrix products  3.65 us (2%)
    all_gather x1, waiting for transfers between devices, on_device(): kv_all = lax.all_gather(kv_pair, 'zc', axis=0, tiled=True)  92.4 us
    pallas_call x1, Pallas kernels, exchange_sum(): pl.pallas_call(functools.partial(exchange_kernel, n), out_shape=jax.Shape...  39.6 us
    all_gather x1, waiting for transfers between devices, on_device(): kv_pair = lax.all_gather(prefix_part, 'xl', axis=0, tiled=True)  27.8 us
    pallas_call x1, Pallas kernels, attend(): pl.pallas_call(functools.partial(attend_kernel, slots), out_shape=jax.Sha...  13.7 us
  transfers between devices with their start and end apart: 2, of which 2 were waited for; matrix products, arithmetic and copies ran while one was open for 3% of the time, Pallas kernels for 0%

profile of v7, /device:TPU:124, one launch (start us, length us, event | category | flops | bytes accessed | tf_op | source)
XLA Modules:
  0.0 201.6 jit_solution(7425152659526905511)
XLA Ops:
  6.5 0.0 copy-start
  6.5 0.0 all-gather.5.cloned.1.call-start
  6.5 3.0 %constant_dynamic-slice_fusion = bf16[8,2,128,1,128]{4,3,2,1,0:T(2,128)(2,1)S(1)} fusion(bf16[8,2,128,4,128]{4,3,2,1,0:T(4,128)(2,1)} %param.9, s32[]{:T(128)S(6)} %select_n.76), kind=kLoop, calls=%fused_computation.36 | loop fusion | bytes 1048580 | tf_op jit(solution)/shard_map/jit(dynamic_index_in_dim)/dynamic_slice | solution.py:210
  9.5 0.9 copy.31
  10.4 0.0 copy-start.3
  10.4 0.0 copy-start.4
  10.4 0.0 copy-start.5
  10.4 0.0 copy-start.1
  10.4 0.0 all-gather.5.cloned.1.call-update
  10.4 0.0 all-gather.7.cloned.1.call-start
  10.5 27.8 %all-gather.5.cloned.1.call-done = bf16[16,2,128,1,128]{4,2,3,1,0:T(8,128)(2,1)} async-done(((bf16[8,2,128,1,128]{4,2,3,1,0:T(8,128)(2,1)}), bf16[16,2,128,1,128]{4,2,3,1,0:T(8,128)(2,1)}) %all-gather.5.cloned.1.call-update) | async-done | bytes 1048592 | tf_op jit(solution)/shard_map/all_gather | solution.py:213
  38.2 0.0 all-gather.7.cloned.1.call-update
  38.3 1.8 constant_dynamic-slice_fusion.1
  40.1 0.0 copy-done.3
  40.1 0.1 copy.25
  40.2 0.1 reduce-window.9
  40.3 0.1 reduce
  40.5 0.0 copy-done.4
  40.5 0.2 fusion
  40.7 0.0 copy-done.5
  40.7 0.2 fusion.1
  40.9 0.3 select_reduce_fusion.2
  41.2 0.0 copy-start.2
  41.2 0.1 fusion.3
  41.3 0.1 select_reduce_fusion.1
  41.4 0.1 compare_select_fusion
  41.4 0.1 select_n.70
  41.5 0.0 copy-done.1
  41.5 0.9 copy.26
  42.4 0.6 fusion.6.ids_ref
  43.0 0.7 fusion.7
  43.7 92.4 %all-gather.7.cloned.1.call-done = bf16[256,2,128,1,128]{4,2,3,1,0:T(8,128)(2,1)} async-done(((bf16[16,2,128,1,128]{4,2,3,1,0:T(8,128)(2,1)}), bf16[256,2,128,1,128]{4,2,3,1,0:T(8,128)(2,1)}) %all-gather.7.cloned.1.call-update) | async-done | bytes 16777232 | tf_op jit(solution)/shard_map/all_gather | solution.py:214
  136.1 0.0 copy-done.2
  136.1 13.7 %shard_map.73 = bf16[2,1024,128]{2,1,0:T(8,128)(2,1)} custom-call(s32[192]{0:T(256)} %fusion.6.ids_ref, s32[2]{0:T(128)} %copy-done.2, bf16[2,1024,128]{2,1,0:T(8,128)(2,1)} %bitcast.32, bf16[2,256,128]{2,1,0:T(8,128)(2,1)} %bitcast.36, bf16[2,256,128]{2,1,0:T(8,128)(2,1)} %bitcast.35, bf16[256,2,128,128]{3,2,1,0:T(8,128)(2,1)} %bitcast.31), custom_call_target="tpu_custom_call" | custom-call | tf_op jit(solution)/shard_map/pallas_call | solution.py:134
  149.8 0.0 copy-done
  149.8 3.7 %bitcast_convert_fusion = bf16[2,256,2048]{2,1,0:T(8,128)(2,1)} fusion(bf16[2,4,256,128]{3,2,1,0:T(8,128)(2,1)} %bitcast.37, bf16[4,128,2048,1]{2,1,0,3:T(8,128)(2,1)S(1)} %bitcast.30), kind=kOutput, calls=%fused_computation | convolution fusion | flops 1074790400 | bytes 4718592 | tf_op jit(solution)/shard_map/dot_general | solution.py:228
  153.5 39.6 %shard_map.74 = bf16[64,2048]{1,0:T(8,128)(2,1)} custom-call(bf16[8,64,2048]{2,1,0:T(8,128)(2,1)} %bitcast.33), custom_call_target="tpu_custom_call" | custom-call | tf_op jit(solution)/shard_map/pallas_call | solution.py:189
  193.1 1.7 copy.35
  (9 shorter events, 0.1 us)
Async XLA Ops:
  6.5 143.3 %copy-start = (bf16[512,2048]{1,0:T(8,128)(2,1)S(1)}, bf16[512,2048]{1,0:T(8,128)(2,1)}, u32[]{:S(2)}) copy-start(bf16[512,2048]{1,0:T(8,128)(2,1)} %param.10) | copy-start | bytes 6291460
  6.5 31.7 %all-gather.5.cloned.1.call-start = ((), (), s32[]{:S(2)}) async-start(), calls=%async_computation | async-start | bytes 1572864 | tf_op jit(solution)/shard_map/all_gather | solution.py:213
  10.4 29.7 %copy-start.3 = (s32[84]{0:T(128)S(1)}, s32[84]{0:T(128)}, u32[]{:S(2)}) copy-start(s32[84]{0:T(128)} %param.11) | copy-start | bytes 1012
  10.4 30.1 %copy-start.4 = (s32[64]{0:T(128)S(1)}, s32[64]{0:T(128)}, u32[]{:S(2)}) copy-start(s32[64]{0:T(128)} %param.13) | copy-start | bytes 772
  10.4 30.3 %copy-start.5 = (s32[16]{0:T(128)S(1)}, s32[16]{0:T(128)}, u32[]{:S(2)}) copy-start(s32[16]{0:T(128)} %param.12) | copy-start | bytes 196
  10.4 31.1 %copy-start.1 = (bf16[512,4,128]{2,1,0:T(4,128)(2,1)S(1)}, bf16[512,4,128]{2,1,0:T(4,128)(2,1)}, u32[]{:S(2)}) copy-start(bf16[512,4,128]{2,1,0:T(4,128)(2,1)} %param.7) | copy-start | bytes 1572868
  10.4 125.7 %all-gather.7.cloned.1.call-start = ((), (), s32[]{:S(2)}) async-start(), calls=%async_computation.1 | async-start | bytes 17825792 | tf_op jit(solution)/shard_map/all_gather | solution.py:214
  41.2 94.9 %copy-start.2 = (s32[2]{0:T(128)}, s32[2]{0:T(128)S(1)}, u32[]{:S(2)}) copy-start(s32[2]{0:T(128)S(1)} %get-tuple-element.11.cnt_ref) | copy-start | bytes 28
Sparse Core Ops, SparseCore 0:
  10.5 27.6 all-gather.4
  40.1 96.0 all-gather.6

commit v8 on v6

--- a/solution.py
+++ b/solution.py
@@ -48,23 +48,56 @@
     return ids.astype(jnp.int32), total.astype(jnp.int32)
 
 
-def attend_kernel(slots, ids_ref, cnt_ref, q_ref, ks_ref, vs_ref, kv_hbm, o_ref, kbuf, vbuf, sem, m_sc, l_sc, acc_sc):
+def suffix_kernel(q_ref, ks_ref, vs_ref, m_ref, l_ref, acc_ref):
+    hd = q_ref.shape[-1]
+    contract = (((1,), (1,)), ((), ()))
+    scores = lax.dot_general(q_ref[...], ks_ref[...], contract, preferred_element_type=jnp.float32)
+    scores = scores * hd ** (-0.5)
+    tok = lax.broadcasted_iota(jnp.int32, scores.shape, 0) % SUFFIX
+    key = lax.broadcasted_iota(jnp.int32, scores.shape, 1)
+    scores = jnp.where(key <= tok, scores, NEG)
+    high = jnp.max(scores, axis=-1, keepdims=True)
+    weights = jnp.exp(scores - high)
+    m_ref[...] = high
+    l_ref[...] = jnp.sum(weights, axis=-1, keepdims=True)
+    acc_ref[...] = jnp.dot(weights.astype(jnp.bfloat16), vs_ref[...], preferred_element_type=jnp.float32)
+
+
+def suffix_attend(q, ks, vs):
+    req, rows, hd = q.shape
+    index = lambda j: (j, 0, 0)
+    return pl.pallas_call(
+        suffix_kernel,
+        out_shape=(
+            jax.ShapeDtypeStruct((req, rows, 1), jnp.float32),
+            jax.ShapeDtypeStruct((req, rows, 1), jnp.float32),
+            jax.ShapeDtypeStruct((req, rows, hd), jnp.float32),
+        ),
+        grid=(req,),
+        in_specs=[
+            pl.BlockSpec((None, rows, hd), index),
+            pl.BlockSpec((None, SUFFIX, hd), index),
+            pl.BlockSpec((None, SUFFIX, hd), index),
+        ],
+        out_specs=[
+            pl.BlockSpec((None, rows, 1), index),
+            pl.BlockSpec((None, rows, 1), index),
+            pl.BlockSpec((None, rows, hd), index),
+        ],
+        compiler_params=pltpu.CompilerParams(dimension_semantics=("arbitrary",)),
+    )(q, ks, vs)
+
+
+def attend_kernel(slots, ids_ref, cnt_ref, q_ref, m0_ref, l0_ref, acc0_ref, kv_hbm, o_ref, kbuf, vbuf, sem, m_sc, l_sc, acc_sc):
     j = pl.program_id(0)
     n = cnt_ref[j]
     rows, hd = q_ref.shape
     scale = hd ** (-0.5)
     contract = (((1,), (1,)), ((), ()))
     q = q_ref[...]
-
-    scores = lax.dot_general(q, ks_ref[...], contract, preferred_element_type=jnp.float32) * scale
-    tok = lax.broadcasted_iota(jnp.int32, scores.shape, 0) % SUFFIX
-    key = lax.broadcasted_iota(jnp.int32, scores.shape, 1)
-    scores = jnp.where(key <= tok, scores, NEG)
-    high = jnp.max(scores, axis=-1, keepdims=True)
-    weights = jnp.exp(scores - high)
-    m_sc[...] = high
-    l_sc[...] = jnp.sum(weights, axis=-1, keepdims=True)
-    acc_sc[...] = jnp.dot(weights.astype(jnp.bfloat16), vs_ref[...], preferred_element_type=jnp.float32)
+    m_sc[...] = m0_ref[...]
+    l_sc[...] = l0_ref[...]
+    acc_sc[...] = acc0_ref[...]
 
     rows_blk = kbuf.shape[1] // GROUP
     steps = (n + GROUP - 1) // GROUP
@@ -127,7 +160,7 @@
     o_ref[...] = (acc_sc[...] / l_sc[...]).astype(o_ref.dtype)
 
 
-def attend(ids, counts, q, ks, vs, kv_all):
+def attend(ids, counts, q, state, kv_all):
     req, rows, hd = q.shape
     slots = ids.shape[1]
     block_shape = kv_all.shape[1:]
@@ -139,8 +172,9 @@
             grid=(req,),
             in_specs=[
                 pl.BlockSpec((None, rows, hd), lambda j, ids, cnt: (j, 0, 0)),
-                pl.BlockSpec((None, SUFFIX, hd), lambda j, ids, cnt: (j, 0, 0)),
-                pl.BlockSpec((None, SUFFIX, hd), lambda j, ids, cnt: (j, 0, 0)),
+                pl.BlockSpec((None, rows, 1), lambda j, ids, cnt: (j, 0, 0)),
+                pl.BlockSpec((None, rows, 1), lambda j, ids, cnt: (j, 0, 0)),
+                pl.BlockSpec((None, rows, hd), lambda j, ids, cnt: (j, 0, 0)),
                 pl.BlockSpec(memory_space=pl.ANY),
             ],
             out_specs=pl.BlockSpec((None, rows, hd), lambda j, ids, cnt: (j, 0, 0)),
@@ -154,7 +188,7 @@
             ],
         ),
         compiler_params=pltpu.CompilerParams(dimension_semantics=("arbitrary",)),
-    )(ids.reshape(-1), counts, q, ks, vs, kv_all)
+    )(ids.reshape(-1), counts, q, *state, kv_all)
 
 
 def exchange_kernel(n, x_ref, o_ref, recv, send_sem, recv_sem):
@@ -218,7 +252,7 @@
     q = q.reshape(req_local, heads_dev * SUFFIX, head_dim)
     ks = suffix_part[:, 0].reshape(req_local, SUFFIX, head_dim)
     vs = suffix_part[:, 1].reshape(req_local, SUFFIX, head_dim)
-    attended = attend(ids, counts, q, ks, vs, kv_all)
+    attended = attend(ids, counts, q, suffix_attend(q, ks, vs), kv_all)
     attended = attended.reshape(req_local, heads_dev, SUFFIX, head_dim)
     w = out_weight.reshape(heads_dev, head_dim, out_weight.shape[1])
     partial = lax.dot_general(

time: 179 us -> 183 us (1.022)
  the two profiles are of different devices: /device:TPU:250 before, /device:TPU:124 now
where the time goes in v8:
time: 183 us
  waiting for transfers between devices  93.9 us (51%)
  Pallas kernels  60.7 us (33%)
  between operations  13.5 us (7%)
  local copies, waits for them, and re-layouts  9.71 us (5%)
  matrix products  3.65 us (2%)
    all_gather x1, waiting for transfers between devices, on_device(): kv_all = lax.all_gather(prefix_part, 'grp', axis=0, tiled=True)  93.9 us
    pallas_call x1, Pallas kernels, attend(): pl.pallas_call(functools.partial(attend_kernel, slots), out_shape=jax.Sha...  32.5 us
    pallas_call x1, Pallas kernels, exchange_sum(): pl.pallas_call(functools.partial(exchange_kernel, n), out_shape=jax.Shape...  24.9 us
  transfers between devices with their start and end apart: 1, of which 1 were waited for; matrix products, arithmetic and copies ran while one was open for 3% of the time, Pallas kernels for 2%

profile of v8, /device:TPU:124, one launch (start us, length us, event | category | flops | bytes accessed | tf_op | source)
XLA Modules:
  0.0 182.7 jit_solution(9949757782618226819)
XLA Ops:
  6.5 0.0 copy-start
  6.5 0.0 all-gather.3.cloned.1.call-start
  6.5 0.0 copy-start.3
  6.5 0.0 copy-start.4
  6.5 0.0 copy-start.5
  6.6 0.0 copy-start.1
  6.6 3.0 %constant_dynamic-slice_fusion = bf16[8,2,128,1,128]{4,3,2,1,0:T(2,128)(2,1)S(1)} fusion(bf16[8,2,128,4,128]{4,3,2,1,0:T(4,128)(2,1)} %param.9, s32[]{:T(128)S(6)} %select_n.50), kind=kLoop, calls=%fused_computation.23 | loop fusion | bytes 1048580 | tf_op jit(solution)/shard_map/jit(dynamic_index_in_dim)/dynamic_slice | solution.py:244
  9.5 0.9 copy.31
  10.5 0.0 all-gather.3.cloned.1.call-update
  10.5 0.0 copy-done.3
  10.5 0.1 copy.25
  10.6 0.1 reduce-window.9
  10.7 0.1 reduce
  10.9 0.0 copy-done.4
  10.9 0.2 fusion
  11.1 0.0 copy-done.5
  11.1 0.2 fusion.1
  11.3 0.3 select_reduce_fusion.2
  11.6 0.0 copy-start.2
  11.6 0.1 fusion.3
  11.7 0.1 select_reduce_fusion.1
  11.7 0.1 compare_select_fusion
  11.8 0.7 select_n.48.ids_ref
  12.5 0.0 copy-done.1
  12.5 0.9 copy.26
  13.3 1.8 constant_dynamic-slice_fusion.1
  15.2 0.7 fusion.4
  15.9 3.4 %shard_map.73 = (f32[2,1024,1]{2,1,0:T(8,128)}, f32[2,1024,1]{2,1,0:T(8,128)}, f32[2,1024,128]{2,1,0:T(8,128)}) custom-call(bf16[2,1024,128]{2,1,0:T(8,128)(2,1)} %bitcast.32, bf16[2,256,128]{2,1,0:T(8,128)(2,1)} %bitcast.39, bf16[2,256,128]{2,1,0:T(8,128)(2,1)} %bitcast.38), custom_call_target="tpu_custom_call" | custom-call | tf_op jit(solution)/shard_map/pallas_call | solution.py:69
  19.2 0.0 copy-done.2
  19.2 93.9 %all-gather.3.cloned.1.call-done = bf16[256,2,128,1,128]{4,2,3,1,0:T(8,128)(2,1)} async-done(((bf16[8,2,128,1,128]{4,2,3,1,0:T(8,128)(2,1)}), bf16[256,2,128,1,128]{4,2,3,1,0:T(8,128)(2,1)}) %all-gather.3.cloned.1.call-update) | async-done | bytes 16777232 | tf_op jit(solution)/shard_map/all_gather | solution.py:246
  113.2 32.5 %shard_map.74 = bf16[2,1024,128]{2,1,0:T(8,128)(2,1)} custom-call(s32[192]{0:T(256)} %select_n.48.ids_ref, s32[2]{0:T(128)} %copy-done.2, bf16[2,1024,128]{2,1,0:T(8,128)(2,1)} %bitcast.33, f32[2,1024,1]{2,1,0:T(8,128)} %get-tuple-element.8.m0_ref, f32[2,1024,1]{2,1,0:T(8,128)} %get-tuple-element.9.l0_ref, f32[2,1024,128]{2,1,0:T(8,128)} %get-tuple-element.10.acc0_ref, ...), custom_call_target="tpu_custom_call" | custom-call | tf_op jit(solution)/shard_map/pallas_call | solution.py:167
  145.7 0.0 copy-done
  145.7 3.7 %bitcast_convert_fusion = bf16[2,256,2048]{2,1,0:T(8,128)(2,1)} fusion(bf16[2,4,256,128]{3,2,1,0:T(8,128)(2,1)} %bitcast.36, bf16[4,128,2048,1]{2,1,0,3:T(8,128)(2,1)S(1)} %bitcast.30), kind=kOutput, calls=%fused_computation | convolution fusion | flops 1074790400 | bytes 4718592 | tf_op jit(solution)/shard_map/dot_general | solution.py:258
  149.3 24.9 %shard_map.75 = bf16[64,2048]{1,0:T(8,128)(2,1)} custom-call(bf16[8,64,2048]{2,1,0:T(8,128)(2,1)} %bitcast.34), custom_call_target="tpu_custom_call" | custom-call | tf_op jit(solution)/shard_map/pallas_call | solution.py:223
  174.2 1.7 copy.35
  (9 shorter events, 0.1 us)
Async XLA Ops:
  6.5 139.1 %copy-start = (bf16[512,2048]{1,0:T(8,128)(2,1)S(1)}, bf16[512,2048]{1,0:T(8,128)(2,1)}, u32[]{:S(2)}) copy-start(bf16[512,2048]{1,0:T(8,128)(2,1)} %param.10) | copy-start | bytes 6291460
  6.5 106.6 %all-gather.3.cloned.1.call-start = ((), (), s32[]{:S(2)}) async-start(), calls=%async_computation | async-start | bytes 17301504 | tf_op jit(solution)/shard_map/all_gather | solution.py:246
  6.5 3.9 %copy-start.3 = (s32[84]{0:T(128)S(1)}, s32[84]{0:T(128)}, u32[]{:S(2)}) copy-start(s32[84]{0:T(128)} %param.11) | copy-start | bytes 1012
  6.5 4.3 %copy-start.4 = (s32[64]{0:T(128)S(1)}, s32[64]{0:T(128)}, u32[]{:S(2)}) copy-start(s32[64]{0:T(128)} %param.13) | copy-start | bytes 772
  6.5 4.5 %copy-start.5 = (s32[16]{0:T(128)S(1)}, s32[16]{0:T(128)}, u32[]{:S(2)}) copy-start(s32[16]{0:T(128)} %param.12) | copy-start | bytes 196
  6.6 5.9 %copy-start.1 = (bf16[512,4,128]{2,1,0:T(4,128)(2,1)S(1)}, bf16[512,4,128]{2,1,0:T(4,128)(2,1)}, u32[]{:S(2)}) copy-start(bf16[512,4,128]{2,1,0:T(4,128)(2,1)} %param.7) | copy-start | bytes 1572868
  11.6 7.7 %copy-start.2 = (s32[2]{0:T(128)}, s32[2]{0:T(128)S(1)}, u32[]{:S(2)}) copy-start(s32[2]{0:T(128)S(1)} %get-tuple-element.17.cnt_ref) | copy-start | bytes 28
Sparse Core Ops, SparseCore 0:
  10.6 102.5 all-gather.2

commit v9 on v8

--- a/solution.py
+++ b/solution.py
@@ -191,18 +191,32 @@
     )(ids.reshape(-1), counts, q, *state, kv_all)
 
 
-def exchange_kernel(n, x_ref, o_ref, recv, send_sem, recv_sem):
+def exchange_kernel(n, a_ref, w_ref, o_ref, send, recv, send_sem, recv_sem):
     me = lax.axis_index("mem")
     grp = lax.axis_index("grp")
+    heads, hd, cols = w_ref.shape
+    rows = o_ref.shape[0]
+    per_req = a_ref.shape[1] // heads // rows
     barrier = pltpu.get_barrier_semaphore()
     for k in range(1, n):
         pl.semaphore_signal(barrier, inc=1, device_id=(grp, lax.rem(me + k, n)), device_id_type=MESH)
     pl.semaphore_wait(barrier, n - 1)
+
+    def chunk(peer):
+        req = peer // per_req
+        first = pl.multiple_of((peer % per_req) * rows, rows)
+        total = jnp.zeros((rows, cols), jnp.float32)
+        for h in range(heads):
+            piece = a_ref[req, pl.ds(h * per_req * rows + first, rows), :]
+            total = total + jnp.dot(piece, w_ref[h], preferred_element_type=jnp.float32)
+        return total.astype(o_ref.dtype)
+
     copies = []
     for k in range(1, n):
         peer = lax.rem(me + k, n)
+        send[k] = chunk(peer)
         copy = pltpu.make_async_remote_copy(
-            src_ref=x_ref.at[peer],
+            src_ref=send.at[k],
             dst_ref=recv.at[k],
             send_sem=send_sem.at[k],
             recv_sem=recv_sem.at[k],
@@ -211,27 +225,29 @@
         )
         copy.start()
         copies.append(copy)
-    total = x_ref[me].astype(jnp.float32)
+    total = chunk(me).astype(jnp.float32)
     for k in range(1, n):
         copies[k - 1].wait()
         total = total + recv[k].astype(jnp.float32)
     o_ref[...] = total.astype(o_ref.dtype)
 
 
-def exchange_sum(x):
-    n, rows, cols = x.shape
+def exchange_sum(n, attended, w):
+    heads, hd, cols = w.shape
+    rows = attended.shape[0] * attended.shape[1] // heads // n
     return pl.pallas_call(
         functools.partial(exchange_kernel, n),
-        out_shape=jax.ShapeDtypeStruct((rows, cols), x.dtype),
-        in_specs=[pl.BlockSpec(memory_space=pltpu.VMEM)],
+        out_shape=jax.ShapeDtypeStruct((rows, cols), jnp.bfloat16),
+        in_specs=[pl.BlockSpec(memory_space=pltpu.VMEM)] * 2,
         out_specs=pl.BlockSpec(memory_space=pltpu.VMEM),
         scratch_shapes=[
-            pltpu.VMEM((n, rows, cols), x.dtype),
+            pltpu.VMEM((n, rows, cols), jnp.bfloat16),
+            pltpu.VMEM((n, rows, cols), jnp.bfloat16),
             pltpu.SemaphoreType.DMA((n,)),
             pltpu.SemaphoreType.DMA((n,)),
         ],
         compiler_params=pltpu.CompilerParams(collective_id=0, has_side_effects=True),
-    )(x)
+    )(attended, w)
 
 
 def on_device(n_mem, queries, suffix_kv, prefix_kv, out_weight, node_blocks, root_of, mid_of):
@@ -253,14 +269,8 @@
     ks = suffix_part[:, 0].reshape(req_local, SUFFIX, head_dim)
     vs = suffix_part[:, 1].reshape(req_local, SUFFIX, head_dim)
     attended = attend(ids, counts, q, suffix_attend(q, ks, vs), kv_all)
-    attended = attended.reshape(req_local, heads_dev, SUFFIX, head_dim)
     w = out_weight.reshape(heads_dev, head_dim, out_weight.shape[1])
-    partial = lax.dot_general(
-        attended, w, (((1, 3), (0, 1)), ((), ())), preferred_element_type=jnp.float32
-    ).astype(jnp.bfloat16)
-    partial = partial.reshape(tokens_dev, out_weight.shape[1])
-    partial = partial.reshape(n_mem, tokens_dev // n_mem, out_weight.shape[1])
-    return exchange_sum(partial)
+    return exchange_sum(n_mem, attended, w)
 
 
 def solution(mesh):

time: 183 us -> 174 us (0.951)
  the two profiles are of different devices: /device:TPU:124 before, /device:TPU:122 now
where the time goes in v9:
time: 174 us; the launch traced here: 173 us
  waiting for transfers between devices  93.9 us (54%)
  Pallas kernels  55.3 us (32%)
  between operations  13.5 us (8%)
  local copies, waits for them, and re-layouts  9.55 us (5%)
    all_gather x1, waiting for transfers between devices, on_device(): kv_all = lax.all_gather(prefix_part, 'grp', axis=0, tiled=True)  93.9 us
    pallas_call x1, Pallas kernels, exchange_sum(): pl.pallas_call(functools.partial(exchange_kernel, n), out_shape=jax.Shape...  40.9 us
    pallas_call x1, Pallas kernels, attend(): pl.pallas_call(functools.partial(attend_kernel, slots), out_shape=jax.Sha...  11 us
    unnamed x15, local copies, waits for them, and re-layouts  4.23 us
  transfers between devices with their start and end apart: 1, of which 1 were waited for; matrix products, arithmetic and copies ran while one was open for 3% of the time, Pallas kernels for 2%

profile of v9, /device:TPU:122, one launch (start us, length us, event | category | flops | bytes accessed | tf_op | source)
XLA Modules:
  0.0 173.4 jit_solution(16045044701531844496)
XLA Ops:
  6.5 0.0 copy-start
  6.5 0.0 all-gather.3.cloned.1.call-start
  6.5 1.6 copy-done
  8.1 0.0 copy-start.3
  8.1 0.0 copy-start.4
  8.1 0.0 copy-start.5
  8.1 0.0 copy-start.1
  8.1 1.2 constant_dynamic-slice_fusion
  9.4 0.9 copy.30
  10.3 0.0 all-gather.3.cloned.1.call-update
  10.3 0.0 copy-done.3
  10.3 0.1 copy.25
  10.4 0.1 reduce-window.9
  10.6 0.1 reduce
  10.7 0.0 copy-done.4
  10.7 0.2 fusion
  10.9 0.0 copy-done.5
  10.9 0.2 fusion.1
  11.1 0.3 select_reduce_fusion.2
  11.4 0.0 copy-start.2
  11.4 0.1 fusion.3
  11.5 0.1 select_reduce_fusion.1
  11.6 0.1 compare_select_fusion
  11.6 0.7 select_n.48.ids_ref
  12.3 0.0 copy-done.1
  12.3 0.9 copy.26
  13.2 1.8 %constant_dynamic-slice_fusion.1 = bf16[512,2,1,128]{3,2,1,0:T(2,128)(2,1)S(1)} fusion(bf16[512,2,4,128]{3,2,1,0:T(4,128)(2,1)} %param.8, s32[]{:T(128)S(6)} %select_n.50), kind=kLoop, calls=%fused_computation.23 | loop fusion | bytes 524292 | tf_op jit(solution)/shard_map/jit(dynamic_index_in_dim)/dynamic_slice | solution.py:261
  15.0 0.7 fusion.4
  15.7 3.4 %shard_map.73 = (f32[2,1024,1]{2,1,0:T(8,128)}, f32[2,1024,1]{2,1,0:T(8,128)}, f32[2,1024,128]{2,1,0:T(8,128)}) custom-call(bf16[2,1024,128]{2,1,0:T(8,128)(2,1)} %bitcast.22, bf16[2,256,128]{2,1,0:T(8,128)(2,1)} %bitcast.28, bf16[2,256,128]{2,1,0:T(8,128)(2,1)} %bitcast.27), custom_call_target="tpu_custom_call" | custom-call | tf_op jit(solution)/shard_map/pallas_call | solution.py:69
  19.1 0.0 copy-done.2
  19.1 93.9 %all-gather.3.cloned.1.call-done = bf16[256,2,128,1,128]{4,2,3,1,0:T(8,128)(2,1)} async-done(((bf16[8,2,128,1,128]{4,2,3,1,0:T(8,128)(2,1)}), bf16[256,2,128,1,128]{4,2,3,1,0:T(8,128)(2,1)}) %all-gather.3.cloned.1.call-update) | async-done | bytes 16777232 | tf_op jit(solution)/shard_map/all_gather | solution.py:262
  112.9 11.0 %shard_map.74.a_ref = bf16[2,1024,128]{2,1,0:T(8,128)(2,1)} custom-call(s32[192]{0:T(256)} %select_n.48.ids_ref, s32[2]{0:T(128)} %copy-done.2, bf16[2,1024,128]{2,1,0:T(8,128)(2,1)} %bitcast.23, f32[2,1024,1]{2,1,0:T(8,128)} %get-tuple-element.8.m0_ref, f32[2,1024,1]{2,1,0:T(8,128)} %get-tuple-element.9.l0_ref, f32[2,1024,128]{2,1,0:T(8,128)} %get-tuple-element.10.acc0_ref, ...), custom_call_target="tpu_custom_call" | custom-call | tf_op jit(solution)/shard_map/pallas_call | solution.py:167
  124.0 40.9 %shard_map.75 = bf16[64,2048]{1,0:T(8,128)(2,1)} custom-call(bf16[2,1024,128]{2,1,0:T(8,128)(2,1)} %shard_map.74.a_ref, bf16[4,128,2048]{2,1,0:T(8,128)(2,1)} %bitcast.24), custom_call_target="tpu_custom_call" | custom-call | tf_op jit(solution)/shard_map/pallas_call | solution.py:238
  164.9 1.7 copy.34
  (9 shorter events, 0.1 us)
Async XLA Ops:
  6.5 1.6 copy-start
  6.5 106.4 %all-gather.3.cloned.1.call-start = ((), (), s32[]{:S(2)}) async-start(), calls=%async_computation | async-start | bytes 17301504 | tf_op jit(solution)/shard_map/all_gather | solution.py:262
  8.1 2.2 %copy-start.3 = (s32[84]{0:T(128)S(1)}, s32[84]{0:T(128)}, u32[]{:S(2)}) copy-start(s32[84]{0:T(128)} %param.11) | copy-start | bytes 1012
  8.1 2.6 %copy-start.4 = (s32[64]{0:T(128)S(1)}, s32[64]{0:T(128)}, u32[]{:S(2)}) copy-start(s32[64]{0:T(128)} %param.13) | copy-start | bytes 772
  8.1 2.8 %copy-start.5 = (s32[16]{0:T(128)S(1)}, s32[16]{0:T(128)}, u32[]{:S(2)}) copy-start(s32[16]{0:T(128)} %param.12) | copy-start | bytes 196
  8.1 4.2 %copy-start.1 = (bf16[512,4,128]{2,1,0:T(4,128)(2,1)S(1)}, bf16[512,4,128]{2,1,0:T(4,128)(2,1)}, u32[]{:S(2)}) copy-start(bf16[512,4,128]{2,1,0:T(4,128)(2,1)} %param.7) | copy-start | bytes 1572868
  11.4 7.7 %copy-start.2 = (s32[2]{0:T(128)}, s32[2]{0:T(128)S(1)}, u32[]{:S(2)}) copy-start(s32[2]{0:T(128)S(1)} %get-tuple-element.17.cnt_ref) | copy-start | bytes 28
Sparse Core Ops, SparseCore 0:
  10.4 102.4 all-gather.2

commit v10 on v9

--- a/solution.py
+++ b/solution.py
@@ -257,7 +257,8 @@
     req_local = tokens_dev // SUFFIX
     group_size = QH // KVH
     kv_start = head_index * heads_dev // group_size
-    prefix_part = lax.dynamic_index_in_dim(prefix_kv, kv_start, 3, keepdims=False)
+    heads_kv = jnp.arange(prefix_kv.shape[3])[None, None, None, :, None]
+    prefix_part = jnp.sum(jnp.where(heads_kv == kv_start, prefix_kv, jnp.zeros_like(prefix_kv)), axis=3)
     suffix_part = lax.dynamic_index_in_dim(suffix_kv, kv_start, 2, keepdims=False)
     kv_all = lax.all_gather(prefix_part, "grp", axis=0, tiled=True)
 

time: 174 us -> 178 us (1.023)
  the two profiles are of different devices: /device:TPU:122 before, /device:TPU:92 now
where the time goes in v10:
time: 178 us
  waiting for transfers between devices  94.3 us (53%)
  Pallas kernels  58.3 us (33%)
  between operations  13.5 us (8%)
  other arithmetic  6.78 us (4%)
  local copies, waits for them, and re-layouts  4.61 us (3%)
    all_gather x1, waiting for transfers between devices, on_device(): kv_all = lax.all_gather(prefix_part, 'grp', axis=0, tiled=True)  94.3 us
    pallas_call x1, Pallas kernels, exchange_sum(): pl.pallas_call(functools.partial(exchange_kernel, n), out_shape=jax.Shape...  41.3 us
    pallas_call x1, Pallas kernels, attend(): pl.pallas_call(functools.partial(attend_kernel, slots), out_shape=jax.Sha...  13.6 us
    reduce_sum x1, other arithmetic, on_device(): jnp.sum(jnp.where(heads_kv == kv_start, prefix_kv, jnp.zeros_like(prefix_...  5.63 us
  transfers between devices with their start and end apart: 1, of which 1 were waited for; matrix products, arithmetic and copies ran while one was open for 2% of the time, Pallas kernels for 2%

profile of v10, /device:TPU:92, one launch (start us, length us, event | category | flops | bytes accessed | tf_op | source)
XLA Modules:
  0.0 177.6 jit_solution(15861376865830551664)
XLA Ops:
  6.5 0.0 copy-start
  6.5 0.0 copy-start.3
  6.5 0.0 copy-start.4
  6.5 0.0 copy-start.5
  6.5 0.0 all-gather.2.cloned.1.call-start
  6.6 0.0 copy-start.1
  6.6 5.6 %select_reduce_fusion = bf16[8,2,128,128]{3,2,1,0:T(8,128)(2,1)} fusion(bf16[8,2,128,4,128]{4,3,2,1,0:T(4,128)(2,1)} %param.9, pred[4]{0:T(512)(128)(4,1)S(1)} %iota_compare_fusion.2), kind=kLoop, calls=%fused_computation | loop fusion | flops 1835008 | bytes 2621444 | tf_op jit(solution)/shard_map/reduce_sum | solution.py:261
  12.3 0.0 all-gather.2.cloned.1.call-update
  12.3 0.0 copy-done.3
  12.3 0.1 copy.22
  12.4 0.1 reduce-window.9
  12.5 0.1 reduce.1
  12.7 0.0 copy-done.4
  12.7 0.2 fusion
  12.9 0.0 copy-done.5
  12.9 0.2 fusion.1
  13.1 0.3 select_reduce_fusion.3
  13.4 0.0 copy-start.2
  13.4 0.1 fusion.3
  13.5 0.1 select_reduce_fusion.2
  13.6 0.1 compare_select_fusion
  13.6 0.7 select_n.50.ids_ref
  14.3 0.0 copy-done
  14.3 0.5 constant_dynamic-slice_fusion
  14.9 0.0 copy-done.1
  14.9 0.9 copy.23
  15.8 0.7 fusion.4
  16.4 3.4 %shard_map.73 = (f32[2,1024,1]{2,1,0:T(8,128)}, f32[2,1024,1]{2,1,0:T(8,128)}, f32[2,1024,128]{2,1,0:T(8,128)}) custom-call(bf16[2,1024,128]{2,1,0:T(8,128)(2,1)} %bitcast.20, bf16[2,256,128]{2,1,0:T(8,128)(2,1)} %bitcast.26, bf16[2,256,128]{2,1,0:T(8,128)(2,1)} %bitcast.25), custom_call_target="tpu_custom_call" | custom-call | tf_op jit(solution)/shard_map/pallas_call | solution.py:69
  19.8 0.0 copy-done.2
  19.8 94.3 %all-gather.2.cloned.1.call-done.kv_hbm = bf16[256,2,128,128]{3,2,1,0:T(8,128)(2,1)} async-done(((bf16[8,2,128,128]{3,2,1,0:T(8,128)(2,1)}), bf16[256,2,128,128]{3,2,1,0:T(8,128)(2,1)}) %all-gather.2.cloned.1.call-update) | async-done | bytes 16777232 | tf_op jit(solution)/shard_map/all_gather | solution.py:263
  114.1 13.6 %shard_map.74.a_ref = bf16[2,1024,128]{2,1,0:T(8,128)(2,1)} custom-call(s32[192]{0:T(256)} %select_n.50.ids_ref, s32[2]{0:T(128)} %copy-done.2, bf16[2,1024,128]{2,1,0:T(8,128)(2,1)} %bitcast.21, f32[2,1024,1]{2,1,0:T(8,128)} %get-tuple-element.8.m0_ref, f32[2,1024,1]{2,1,0:T(8,128)} %get-tuple-element.9.l0_ref, f32[2,1024,128]{2,1,0:T(8,128)} %get-tuple-element.10.acc0_ref, ...), custom_call_target="tpu_custom_call" | custom-call | tf_op jit(solution)/shard_map/pallas_call | solution.py:167
  127.8 41.3 %shard_map.75 = bf16[64,2048]{1,0:T(8,128)(2,1)} custom-call(bf16[2,1024,128]{2,1,0:T(8,128)(2,1)} %shard_map.74.a_ref, bf16[4,128,2048]{2,1,0:T(8,128)(2,1)} %bitcast.22), custom_call_target="tpu_custom_call" | custom-call | tf_op jit(solution)/shard_map/pallas_call | solution.py:238
  169.1 1.7 copy.29
  (10 shorter events, 0.1 us)
Async XLA Ops:
  6.5 7.7 %copy-start = (bf16[512,2,4,128]{3,2,1,0:T(4,128)(2,1)S(1)}, bf16[512,2,4,128]{3,2,1,0:T(4,128)(2,1)}, u32[]{:S(2)}) copy-start(bf16[512,2,4,128]{3,2,1,0:T(4,128)(2,1)} %param.8) | copy-start | bytes 3145732
  6.5 5.8 %copy-start.3 = (s32[84]{0:T(128)S(1)}, s32[84]{0:T(128)}, u32[]{:S(2)}) copy-start(s32[84]{0:T(128)} %param.11) | copy-start | bytes 1012
  6.5 6.1 %copy-start.4 = (s32[64]{0:T(128)S(1)}, s32[64]{0:T(128)}, u32[]{:S(2)}) copy-start(s32[64]{0:T(128)} %param.13) | copy-start | bytes 772
  6.5 6.3 %copy-start.5 = (s32[16]{0:T(128)S(1)}, s32[16]{0:T(128)}, u32[]{:S(2)}) copy-start(s32[16]{0:T(128)} %param.12) | copy-start | bytes 196
  6.5 107.6 %all-gather.2.cloned.1.call-start = ((), (), s32[]{:S(2)}) async-start(), calls=%async_computation | async-start | bytes 17301504 | tf_op jit(solution)/shard_map/all_gather | solution.py:263
  6.6 8.3 %copy-start.1 = (bf16[512,4,128]{2,1,0:T(4,128)(2,1)S(1)}, bf16[512,4,128]{2,1,0:T(4,128)(2,1)}, u32[]{:S(2)}) copy-start(bf16[512,4,128]{2,1,0:T(4,128)(2,1)} %param.7) | copy-start | bytes 1572868
  13.4 6.5 %copy-start.2 = (s32[2]{0:T(128)}, s32[2]{0:T(128)S(1)}, u32[]{:S(2)}) copy-start(s32[2]{0:T(128)S(1)} %get-tuple-element.17.cnt_ref) | copy-start | bytes 28
Sparse Core Ops, SparseCore 0:
  12.4 101.6 all-gather.1

commit v11 on v9

--- a/solution.py
+++ b/solution.py
@@ -11,7 +11,7 @@
 KVH = 4
 SUFFIX = 256
 MOST_BLK = 32
-GROUP = 8
+GROUP = 16
 NEG = -1e30
 MESH = pl.DeviceIdType.MESH
 

time: 174 us -> 192 us (1.10)
  the two profiles are of different devices: /device:TPU:122 before, /device:TPU:124 now
where the time goes in v11:
time: 192 us; the launch traced here: 191 us
  waiting for transfers between devices  93.9 us (49%)
  Pallas kernels  73 us (38%)
  between operations  13.5 us (7%)
  local copies, waits for them, and re-layouts  9.55 us (5%)
    all_gather x1, waiting for transfers between devices, on_device(): kv_all = lax.all_gather(prefix_part, 'grp', axis=0, tiled=True)  93.9 us
    pallas_call x1, Pallas kernels, exchange_sum(): pl.pallas_call(functools.partial(exchange_kernel, n), out_shape=jax.Shape...  41.3 us
    pallas_call x1, Pallas kernels, attend(): pl.pallas_call(functools.partial(attend_kernel, slots), out_shape=jax.Sha...  28.3 us
    unnamed x15, local copies, waits for them, and re-layouts  4.23 us
  transfers between devices with their start and end apart: 1, of which 1 were waited for; matrix products, arithmetic and copies ran while one was open for 3% of the time, Pallas kernels for 2%

profile of v11, /device:TPU:124, one launch (start us, length us, event | category | flops | bytes accessed | tf_op | source)
XLA Modules:
  0.0 191.2 jit_solution(8403652995572433441)
XLA Ops:
  6.5 0.0 copy-start
  6.5 0.0 all-gather.3.cloned.1.call-start
  6.5 1.6 copy-done
  8.1 0.0 copy-start.3
  8.1 0.0 copy-start.4
  8.1 0.0 copy-start.5
  8.1 0.0 copy-start.1
  8.1 1.2 constant_dynamic-slice_fusion
  9.4 0.9 copy.30
  10.3 0.0 all-gather.3.cloned.1.call-update
  10.3 0.0 copy-done.3
  10.3 0.1 copy.25
  10.4 0.1 reduce-window.9
  10.6 0.1 reduce
  10.7 0.0 copy-done.4
  10.7 0.2 fusion
  10.9 0.0 copy-done.5
  10.9 0.2 fusion.1
  11.1 0.3 select_reduce_fusion.2
  11.4 0.0 copy-start.2
  11.4 0.1 fusion.3
  11.5 0.1 select_reduce_fusion.1
  11.6 0.1 compare_select_fusion
  11.6 0.7 select_n.48.ids_ref
  12.3 0.0 copy-done.1
  12.3 0.9 copy.26
  13.2 1.8 constant_dynamic-slice_fusion.1
  15.0 0.7 fusion.4
  15.7 3.4 %shard_map.73 = (f32[2,1024,1]{2,1,0:T(8,128)}, f32[2,1024,1]{2,1,0:T(8,128)}, f32[2,1024,128]{2,1,0:T(8,128)}) custom-call(bf16[2,1024,128]{2,1,0:T(8,128)(2,1)} %bitcast.22, bf16[2,256,128]{2,1,0:T(8,128)(2,1)} %bitcast.28, bf16[2,256,128]{2,1,0:T(8,128)(2,1)} %bitcast.27), custom_call_target="tpu_custom_call" | custom-call | tf_op jit(solution)/shard_map/pallas_call | solution.py:69
  19.1 0.0 copy-done.2
  19.1 93.9 %all-gather.3.cloned.1.call-done = bf16[256,2,128,1,128]{4,2,3,1,0:T(8,128)(2,1)} async-done(((bf16[8,2,128,1,128]{4,2,3,1,0:T(8,128)(2,1)}), bf16[256,2,128,1,128]{4,2,3,1,0:T(8,128)(2,1)}) %all-gather.3.cloned.1.call-update) | async-done | bytes 16777232 | tf_op jit(solution)/shard_map/all_gather | solution.py:262
  113.0 28.3 %shard_map.74.a_ref = bf16[2,1024,128]{2,1,0:T(8,128)(2,1)} custom-call(s32[192]{0:T(256)} %select_n.48.ids_ref, s32[2]{0:T(128)} %copy-done.2, bf16[2,1024,128]{2,1,0:T(8,128)(2,1)} %bitcast.23, f32[2,1024,1]{2,1,0:T(8,128)} %get-tuple-element.8.m0_ref, f32[2,1024,1]{2,1,0:T(8,128)} %get-tuple-element.9.l0_ref, f32[2,1024,128]{2,1,0:T(8,128)} %get-tuple-element.10.acc0_ref, ...), custom_call_target="tpu_custom_call" | custom-call | tf_op jit(solution)/shard_map/pallas_call | solution.py:167
  141.3 41.3 %shard_map.75 = bf16[64,2048]{1,0:T(8,128)(2,1)} custom-call(bf16[2,1024,128]{2,1,0:T(8,128)(2,1)} %shard_map.74.a_ref, bf16[4,128,2048]{2,1,0:T(8,128)(2,1)} %bitcast.24), custom_call_target="tpu_custom_call" | custom-call | tf_op jit(solution)/shard_map/pallas_call | solution.py:238
  182.6 1.7 copy.34
  (9 shorter events, 0.1 us)
Async XLA Ops:
  6.5 1.6 copy-start
  6.5 106.5 %all-gather.3.cloned.1.call-start = ((), (), s32[]{:S(2)}) async-start(), calls=%async_computation | async-start | bytes 17301504 | tf_op jit(solution)/shard_map/all_gather | solution.py:262
  8.1 2.2 %copy-start.3 = (s32[84]{0:T(128)S(1)}, s32[84]{0:T(128)}, u32[]{:S(2)}) copy-start(s32[84]{0:T(128)} %param.11) | copy-start | bytes 1012
  8.1 2.6 %copy-start.4 = (s32[64]{0:T(128)S(1)}, s32[64]{0:T(128)}, u32[]{:S(2)}) copy-start(s32[64]{0:T(128)} %param.13) | copy-start | bytes 772
  8.1 2.8 %copy-start.5 = (s32[16]{0:T(128)S(1)}, s32[16]{0:T(128)}, u32[]{:S(2)}) copy-start(s32[16]{0:T(128)} %param.12) | copy-start | bytes 196
  8.1 4.2 %copy-start.1 = (bf16[512,4,128]{2,1,0:T(4,128)(2,1)S(1)}, bf16[512,4,128]{2,1,0:T(4,128)(2,1)}, u32[]{:S(2)}) copy-start(bf16[512,4,128]{2,1,0:T(4,128)(2,1)} %param.7) | copy-start | bytes 1572868
  11.4 7.7 %copy-start.2 = (s32[2]{0:T(128)}, s32[2]{0:T(128)S(1)}, u32[]{:S(2)}) copy-start(s32[2]{0:T(128)S(1)} %get-tuple-element.17.cnt_ref) | copy-start | bytes 28
Sparse Core Ops, SparseCore 0:
  10.4 102.5 all-gather.2

commit v12 on v9

--- a/solution.py
+++ b/solution.py
@@ -211,9 +211,14 @@
             total = total + jnp.dot(piece, w_ref[h], preferred_element_type=jnp.float32)
         return total.astype(o_ref.dtype)
 
+    n_y = n // 2
+    x_hi, y = me // n_y, me % n_y
+    shifts = [(a, b) for a in range(2) for b in range(n_y) if (a, b) != (0, 0)]
+    shifts.sort(key=lambda ab: -(2 * ab[0] + min(ab[1], n_y - ab[1])))
     copies = []
-    for k in range(1, n):
-        peer = lax.rem(me + k, n)
+    for a, b in shifts:
+        k = a * n_y + b
+        peer = ((x_hi + a) % 2) * n_y + (y + b) % n_y
         send[k] = chunk(peer)
         copy = pltpu.make_async_remote_copy(
             src_ref=send.at[k],
@@ -224,10 +229,10 @@
             device_id_type=MESH,
         )
         copy.start()
-        copies.append(copy)
+        copies.append((k, copy))
     total = chunk(me).astype(jnp.float32)
-    for k in range(1, n):
-        copies[k - 1].wait()
+    for k, copy in copies:
+        copy.wait()
         total = total + recv[k].astype(jnp.float32)
     o_ref[...] = total.astype(o_ref.dtype)
 

time: 174 us -> 181 us (1.040)
  the two profiles are of different devices: /device:TPU:122 before, /device:TPU:129 now
where the time goes in v12:
time: 181 us
  waiting for transfers between devices  92.2 us (51%)
  Pallas kernels  64.2 us (35%)
  between operations  13.5 us (7%)
  local copies, waits for them, and re-layouts  9.55 us (5%)
    all_gather x1, waiting for transfers between devices, on_device(): kv_all = lax.all_gather(prefix_part, 'grp', axis=0, tiled=True)  92.2 us
    pallas_call x1, Pallas kernels, exchange_sum(): pl.pallas_call(functools.partial(exchange_kernel, n), out_shape=jax.Shape...  31 us
    pallas_call x1, Pallas kernels, attend(): pl.pallas_call(functools.partial(attend_kernel, slots), out_shape=jax.Sha...  29.8 us
    unnamed x15, local copies, waits for them, and re-layouts  4.23 us
  transfers between devices with their start and end apart: 1, of which 1 were waited for; matrix products, arithmetic and copies ran while one was open for 3% of the time, Pallas kernels for 2%

profile of v12, /device:TPU:129, one launch (start us, length us, event | category | flops | bytes accessed | tf_op | source)
XLA Modules:
  0.0 180.6 jit_solution(7987470428979779804)
XLA Ops:
  6.5 0.0 copy-start
  6.5 0.0 all-gather.3.cloned.1.call-start
  6.5 1.6 copy-done
  8.1 0.0 copy-start.3
  8.1 0.0 copy-start.4
  8.1 0.0 copy-start.5
  8.1 0.0 copy-start.1
  8.1 1.2 constant_dynamic-slice_fusion
  9.4 0.9 copy.30
  10.3 0.0 all-gather.3.cloned.1.call-update
  10.3 0.0 copy-done.3
  10.3 0.1 copy.25
  10.4 0.1 reduce-window.9
  10.6 0.1 reduce
  10.7 0.0 copy-done.4
  10.7 0.2 fusion
  10.9 0.0 copy-done.5
  10.9 0.2 fusion.1
  11.1 0.3 select_reduce_fusion.2
  11.4 0.0 copy-start.2
  11.4 0.1 fusion.3
  11.5 0.1 select_reduce_fusion.1
  11.6 0.1 compare_select_fusion
  11.6 0.7 select_n.48.ids_ref
  12.3 0.0 copy-done.1
  12.3 0.9 copy.26
  13.2 1.8 constant_dynamic-slice_fusion.1
  15.0 0.7 fusion.4
  15.7 3.4 %shard_map.73 = (f32[2,1024,1]{2,1,0:T(8,128)}, f32[2,1024,1]{2,1,0:T(8,128)}, f32[2,1024,128]{2,1,0:T(8,128)}) custom-call(bf16[2,1024,128]{2,1,0:T(8,128)(2,1)} %bitcast.22, bf16[2,256,128]{2,1,0:T(8,128)(2,1)} %bitcast.28, bf16[2,256,128]{2,1,0:T(8,128)(2,1)} %bitcast.27), custom_call_target="tpu_custom_call" | custom-call | tf_op jit(solution)/shard_map/pallas_call | solution.py:69
  19.1 0.0 copy-done.2
  19.1 92.2 %all-gather.3.cloned.1.call-done = bf16[256,2,128,1,128]{4,2,3,1,0:T(8,128)(2,1)} async-done(((bf16[8,2,128,1,128]{4,2,3,1,0:T(8,128)(2,1)}), bf16[256,2,128,1,128]{4,2,3,1,0:T(8,128)(2,1)}) %all-gather.3.cloned.1.call-update) | async-done | bytes 16777232 | tf_op jit(solution)/shard_map/all_gather | solution.py:267
  111.3 29.8 %shard_map.74.a_ref = bf16[2,1024,128]{2,1,0:T(8,128)(2,1)} custom-call(s32[192]{0:T(256)} %select_n.48.ids_ref, s32[2]{0:T(128)} %copy-done.2, bf16[2,1024,128]{2,1,0:T(8,128)(2,1)} %bitcast.23, f32[2,1024,1]{2,1,0:T(8,128)} %get-tuple-element.8.m0_ref, f32[2,1024,1]{2,1,0:T(8,128)} %get-tuple-element.9.l0_ref, f32[2,1024,128]{2,1,0:T(8,128)} %get-tuple-element.10.acc0_ref, ...), custom_call_target="tpu_custom_call" | custom-call | tf_op jit(solution)/shard_map/pallas_call | solution.py:167
  141.1 31.0 %shard_map.75 = bf16[64,2048]{1,0:T(8,128)(2,1)} custom-call(bf16[2,1024,128]{2,1,0:T(8,128)(2,1)} %shard_map.74.a_ref, bf16[4,128,2048]{2,1,0:T(8,128)(2,1)} %bitcast.24), custom_call_target="tpu_custom_call" | custom-call | tf_op jit(solution)/shard_map/pallas_call | solution.py:243
  172.1 1.7 copy.34
  (9 shorter events, 0.1 us)
Async XLA Ops:
  6.5 1.6 copy-start
  6.5 104.7 %all-gather.3.cloned.1.call-start = ((), (), s32[]{:S(2)}) async-start(), calls=%async_computation | async-start | bytes 17301504 | tf_op jit(solution)/shard_map/all_gather | solution.py:267
  8.1 2.2 %copy-start.3 = (s32[84]{0:T(128)S(1)}, s32[84]{0:T(128)}, u32[]{:S(2)}) copy-start(s32[84]{0:T(128)} %param.11) | copy-start | bytes 1012
  8.1 2.6 %copy-start.4 = (s32[64]{0:T(128)S(1)}, s32[64]{0:T(128)}, u32[]{:S(2)}) copy-start(s32[64]{0:T(128)} %param.13) | copy-start | bytes 772
  8.1 2.8 %copy-start.5 = (s32[16]{0:T(128)S(1)}, s32[16]{0:T(128)}, u32[]{:S(2)}) copy-start(s32[16]{0:T(128)} %param.12) | copy-start | bytes 196
  8.1 4.2 %copy-start.1 = (bf16[512,4,128]{2,1,0:T(4,128)(2,1)S(1)}, bf16[512,4,128]{2,1,0:T(4,128)(2,1)}, u32[]{:S(2)}) copy-start(bf16[512,4,128]{2,1,0:T(4,128)(2,1)} %param.7) | copy-start | bytes 1572868
  11.4 7.7 %copy-start.2 = (s32[2]{0:T(128)}, s32[2]{0:T(128)S(1)}, u32[]{:S(2)}) copy-start(s32[2]{0:T(128)S(1)} %get-tuple-element.17.cnt_ref) | copy-start | bytes 28
Sparse Core Ops, SparseCore 0:
  10.4 100.7 all-gather.2
